TPU v7x, 32 devices: a whole 2x2x4 slice. The times are simulated.
32 devices in a mesh: rep: 4 (over y, x), ep: 8 (over z, core).
Axes of the slice: x: 2, y: 2, z: 4, core: 2. Of those that a mesh axis runs over, the one named last changes fastest.
Arguments:
- tokens_in: bfloat16 [16384, 1024], P(('rep', 'ep')), may hold values from -6 to 6
- token_ids: int32 [16384], P(('rep', 'ep')), may hold values from 0 to 8191, as said below
- hash_table: int32 [8192], replicated, may hold values from 0 to 7, as said below
- doc_lengths: int32 [32, 4], P(('rep', 'ep')), may hold values from 0 to 512, as said below
- gain_one: float32 [1024], replicated, may hold values from 0.5 to 1.5
- shift_one: float32 [1024], replicated, may hold values from -1.2 to 1.2
- project_in: bfloat16 [1024, 3072], replicated, may hold values from -0.1875 to 0.1875
- project_out: bfloat16 [1024, 1024], replicated, may hold values from -0.5 to 0.5
- gain_two: float32 [1024], replicated, may hold values from 0.5 to 1.5
- shift_two: float32 [1024], replicated, may hold values from -1.2 to 1.2
- expert_in: bfloat16 [8, 1024, 4096], P('ep'), may hold values from -0.1875 to 0.1875
- expert_out: bfloat16 [8, 4096, 1024], P('ep'), may hold values from -0.09375 to 0.09375
- out_grad: bfloat16 [16384, 1024], P(('rep', 'ep')), may hold values from -6 to 6
Outputs:
- block_out: bfloat16 [16384, 1024], P(('rep', 'ep'))
- grad_in: float32 [16384, 1024], P(('rep', 'ep'))
- grad_project_in: float32 [1024, 3072], P(('rep', 'ep'))
- grad_project_out: float32 [1024, 1024], P(('rep', 'ep'))
- grad_gain_one: float32 [1024], P(('rep', 'ep'))
- grad_shift_one: float32 [1024], P(('rep', 'ep'))
- grad_gain_two: float32 [1024], P(('rep', 'ep'))
- grad_shift_two: float32 [1024], P(('rep', 'ep'))
- grad_expert_in: float32 [8, 1024, 4096], P('ep', 'rep')
- grad_expert_out: float32 [8, 4096, 1024], P('ep', 'rep')
Inputs may be any that keep to these rules, and one draw needn't show every extreme that they name: `token_ids`: each device's 512 ids send at most 128 tokens to one expert, and on every device some experts get exactly 128. `hash_table`: each expert serves 8192 // 8 ids. `doc_lengths`: each row sums to 512; a 0 is an empty document. Some device holds a single document.
All inputs are finite; a program needn't handle non-finite values.
Results may differ from a plain program's by a relative error of at most 0.012.
Values may be sent and summed in bfloat16 or wider, within the bound.
No kernel may reach another device: no remote copies, remote signals or barrier semaphores. Data moves between devices by JAX's collectives and lax.ppermute only.
A program may use at most 192 MiB of HBM per device.

v0:
```python
import math

import jax
import jax.numpy as jnp
from jax import lax
from jax.sharding import PartitionSpec as P

HEADS = 16


NEG_LARGE = -1e30
EPSILON = 1e-05


def layer_norm(values, gain_vec, shift_vec):
    center = jnp.mean(values, -1, keepdims=True)
    centered = values - center
    spread = jnp.mean(centered * centered, -1, keepdims=True)
    return centered * lax.rsqrt(spread + EPSILON) * gain_vec + shift_vec


def smooth_gate(values):
    return jax.nn.gelu(values, approximate=True)


def document_mask(lengths, length_total):
    bounds = jnp.cumsum(lengths)
    position = jnp.arange(length_total, dtype=jnp.int32)
    doc_index = jnp.sum((position[:, None] >= bounds[None, :]).astype(jnp.int32), 1)
    same_doc = doc_index[:, None] == doc_index[None, :]
    causal = position[:, None] >= position[None, :]
    return jnp.logical_and(same_doc, causal)


def slot_ranks(expert_ids, expert_count):
    one_hot = (expert_ids[:, None] == jnp.arange(expert_count, dtype=jnp.int32)[None, :]).astype(
        jnp.int32
    )
    earlier = jnp.cumsum(one_hot, 0) - one_hot
    return jnp.sum(earlier * one_hot, 1)


def split_heads(matrix, group_count):
    tok_rows = matrix.shape[0]
    return jnp.moveaxis(matrix.reshape(tok_rows, group_count, 4, -1), 1, 0)


def join_heads(pieces):
    regrouped = jnp.moveaxis(pieces, 0, 1)
    return regrouped.reshape(regrouped.shape[0], -1)


def masked_scores(query_part, key_part, attend_mask, score_scale):
    scores = (
        jnp.einsum("qhd,khd->hqk", query_part, key_part, preferred_element_type=jnp.float32)
        * score_scale
    )
    return jnp.where(attend_mask[None], scores, NEG_LARGE)


def attend_forward(query_heads, key_heads, value_heads, attend_mask, score_scale):

    def head_group(members):
        query_part, key_part, value_part = members
        scores = masked_scores(query_part, key_part, attend_mask, score_scale)
        row_max = jnp.max(scores, -1, keepdims=True)
        exponent = jnp.exp(scores - row_max)
        row_total = jnp.sum(exponent, -1, keepdims=True)
        weights_low = (exponent / row_total).astype(jnp.bfloat16)
        mixture = jnp.einsum(
            "hqk,khd->qhd", weights_low, value_part, preferred_element_type=jnp.float32
        )
        return (mixture.astype(jnp.bfloat16), (row_max + jnp.log(row_total))[..., 0])

    return lax.map(head_group, (query_heads, key_heads, value_heads))


def attend_backward(
    query_heads, key_heads, value_heads, grad_heads, log_totals, attend_mask, score_scale
):

    def head_group(members):
        query_part, key_part, value_part, grad_part, total_part = members
        scores = masked_scores(query_part, key_part, attend_mask, score_scale)
        weights = jnp.exp(scores - total_part[..., None])
        grad_weights = jnp.einsum(
            "qhd,khd->hqk", grad_part, value_part, preferred_element_type=jnp.float32
        )
        grad_scores = (
            weights * (grad_weights - jnp.sum(weights * grad_weights, -1, keepdims=True))
        ).astype(jnp.bfloat16)
        grad_query = (
            jnp.einsum("hqk,khd->qhd", grad_scores, key_part, preferred_element_type=jnp.float32)
            * score_scale
        )
        grad_key = (
            jnp.einsum("hqk,qhd->khd", grad_scores, query_part, preferred_element_type=jnp.float32)
            * score_scale
        )
        grad_value = jnp.einsum(
            "hqk,qhd->khd",
            weights.astype(jnp.bfloat16),
            grad_part,
            preferred_element_type=jnp.float32,
        )
        return (grad_query, grad_key, grad_value)

    return lax.map(head_group, (query_heads, key_heads, value_heads, grad_heads, log_totals))


def local(
    tokens_in,
    token_ids,
    hash_table,
    doc_lengths,
    gain_one,
    shift_one,
    project_in,
    project_out,
    gain_two,
    shift_two,
    expert_in,
    expert_out,
    out_grad,
):
    tok_rows, model_width = tokens_in.shape
    group_count = HEADS // 4
    score_scale = 1.0 / math.sqrt(model_width // HEADS)
    expert_count = expert_in.shape[0] * lax.axis_size("ep")
    capacity = 2 * tok_rows // expert_count
    inputs = tokens_in.astype(jnp.float32)
    attend_mask = document_mask(doc_lengths[0], tok_rows)
    normed_one, pull_one = jax.vjp(layer_norm, inputs, gain_one, shift_one)
    normed_one_low = normed_one.astype(jnp.bfloat16)
    joined = jnp.dot(normed_one_low, project_in, preferred_element_type=jnp.float32).astype(
        jnp.bfloat16
    )
    query_heads = split_heads(joined[:, :model_width], group_count)
    key_heads = split_heads(joined[:, model_width : 2 * model_width], group_count)
    value_heads = split_heads(joined[:, 2 * model_width :], group_count)
    mixture_heads, log_totals = attend_forward(
        query_heads, key_heads, value_heads, attend_mask, score_scale
    )
    mixture = join_heads(mixture_heads)
    hidden = inputs + jnp.dot(mixture, project_out, preferred_element_type=jnp.float32)
    normed_two, pull_two = jax.vjp(layer_norm, hidden, gain_two, shift_two)
    routed = normed_two.astype(jnp.bfloat16)
    expert_ids = jnp.take(hash_table, token_ids)
    slot_rank = slot_ranks(expert_ids, expert_count)
    dispatch_buffer = (
        jnp.zeros((expert_count, capacity, model_width), jnp.bfloat16)
        .at[expert_ids, slot_rank]
        .set(routed)
    )
    first_weight = expert_in[0]
    second_weight = expert_out[0]
    received = lax.all_to_all(dispatch_buffer, "ep", split_axis=0, concat_axis=0, tiled=True)
    pre_act = jnp.einsum("scd,df->scf", received, first_weight, preferred_element_type=jnp.float32)
    activation = smooth_gate(pre_act).astype(jnp.bfloat16)
    result = jnp.einsum(
        "scf,fd->scd", activation, second_weight, preferred_element_type=jnp.float32
    ).astype(jnp.bfloat16)
    returned = lax.all_to_all(result, "ep", split_axis=0, concat_axis=0, tiled=True)
    outcome = (returned, received)
    returned = outcome[0]
    received = outcome[1]
    block_sum = hidden + returned[expert_ids, slot_rank].astype(jnp.float32)
    block_out = block_sum.astype(jnp.bfloat16)
    grad_out = out_grad.astype(jnp.float32)
    grad_buffer = (
        jnp.zeros((expert_count, capacity, model_width), jnp.bfloat16)
        .at[expert_ids, slot_rank]
        .set(out_grad)
    )
    grad_received = lax.all_to_all(grad_buffer, "ep", split_axis=0, concat_axis=0, tiled=True)
    pre_act = jnp.einsum("scd,df->scf", received, first_weight, preferred_element_type=jnp.float32)
    gate_value, gate_pull = jax.vjp(smooth_gate, pre_act)
    activation = gate_value.astype(jnp.bfloat16)
    grad_second = jnp.einsum(
        "scf,scd->fd", activation, grad_received, preferred_element_type=jnp.float32
    )
    grad_act = jnp.einsum(
        "scd,fd->scf", grad_received, second_weight, preferred_element_type=jnp.float32
    )
    grad_pre = gate_pull(grad_act)[0].astype(jnp.bfloat16)
    grad_first = jnp.einsum("scd,scf->df", received, grad_pre, preferred_element_type=jnp.float32)
    grad_routed = jnp.einsum(
        "scf,df->scd", grad_pre, first_weight, preferred_element_type=jnp.float32
    ).astype(jnp.bfloat16)
    grad_back = lax.all_to_all(grad_routed, "ep", split_axis=0, concat_axis=0, tiled=True)
    grad_normed_two = grad_back[expert_ids, slot_rank].astype(jnp.float32)
    hidden_part, grad_gain_two, grad_shift_two = pull_two(grad_normed_two)
    grad_hidden = grad_out + hidden_part
    grad_hidden_low = grad_hidden.astype(jnp.bfloat16)
    grad_project_out = jnp.einsum(
        "td,te->de", mixture, grad_hidden_low, preferred_element_type=jnp.float32
    )
    grad_mixture = jnp.einsum(
        "te,de->td", grad_hidden_low, project_out, preferred_element_type=jnp.float32
    ).astype(jnp.bfloat16)
    grad_heads = split_heads(grad_mixture, group_count)
    grad_query, grad_key, grad_value = attend_backward(
        query_heads, key_heads, value_heads, grad_heads, log_totals, attend_mask, score_scale
    )
    grad_joined = jnp.concatenate(
        [join_heads(grad_query), join_heads(grad_key), join_heads(grad_value)], 1
    ).astype(jnp.bfloat16)
    grad_project_in = jnp.einsum(
        "td,te->de", normed_one_low, grad_joined, preferred_element_type=jnp.float32
    )
    grad_normed_one = jnp.einsum(
        "te,de->td", grad_joined, project_in, preferred_element_type=jnp.float32
    )
    input_part, grad_gain_one, grad_shift_one = pull_one(grad_normed_one)
    grad_in = grad_hidden + input_part
    summed_first, summed_second = (
        lax.psum_scatter(
            grad_first[None].astype(jnp.bfloat16), "rep", scatter_dimension=1, tiled=True
        ).astype(jnp.float32),
        lax.psum_scatter(
            grad_second[None].astype(jnp.bfloat16), "rep", scatter_dimension=1, tiled=True
        ).astype(jnp.float32),
    )
    dense_parts = (
        lax.psum_scatter(grad_project_in, ("rep", "ep"), scatter_dimension=0, tiled=True),
        lax.psum_scatter(grad_project_out, ("rep", "ep"), scatter_dimension=0, tiled=True),
        lax.psum_scatter(grad_gain_one, ("rep", "ep"), scatter_dimension=0, tiled=True),
        lax.psum_scatter(grad_shift_one, ("rep", "ep"), scatter_dimension=0, tiled=True),
        lax.psum_scatter(grad_gain_two, ("rep", "ep"), scatter_dimension=0, tiled=True),
        lax.psum_scatter(grad_shift_two, ("rep", "ep"), scatter_dimension=0, tiled=True),
    )
    return (
        block_out,
        grad_in,
        dense_parts[0],
        dense_parts[1],
        dense_parts[2],
        dense_parts[3],
        dense_parts[4],
        dense_parts[5],
        summed_first,
        summed_second,
    )


def solution(mesh):
    in_specs = (
        P(("rep", "ep"), None),
        P(("rep", "ep")),
        P(),
        P(("rep", "ep"), None),
        P(),
        P(),
        P(),
        P(),
        P(),
        P(),
        P("ep", None, None),
        P("ep", None, None),
        P(("rep", "ep"), None),
    )
    out_specs = (
        P(("rep", "ep"), None),
        P(("rep", "ep"), None),
        P(("rep", "ep"), None),
        P(("rep", "ep"), None),
        P(("rep", "ep")),
        P(("rep", "ep")),
        P(("rep", "ep")),
        P(("rep", "ep")),
        P("ep", "rep", None),
        P("ep", "rep", None),
    )
    return jax.shard_map(local, mesh=mesh, in_specs=in_specs, out_specs=out_specs, check_vma=False)
```

profile of v0, /device:TPU:0, one launch (start us, length us, event | category | flops | bytes accessed | tf_op | source)
XLA Modules:
  0.0 789.4 jit_solution(7434811174761907421)
XLA Ops:
  12.7 3.1 gather_fusion
  17.4 6.7 convolution_convert_fusion
  25.9 2.3 copy.59
  28.2 2.3 copy.58
  30.5 2.3 copy.57
  32.7 26.9 %while.28 = (s32[]{:T(128)}, bf16[4,512,4,64]{1,3,2,0:T(8,128)(2,1)}, f32[4,4,512]{2,1,0:T(4,128)}, bf16[4,512,4,64]{1,3,2,0:T(8,128)(2,1)}, bf16[4,512,4,64]{1,...) while((s32[]{:T(128)}, ...), condition=%wide.region_7.8_spmd.clone, body=%wide.region_4.7_spmd.clone.sunk | while | flops 281933824 | bytes 14749793 | solution.py:75
  33.0 1.9 fusion.156
  35.8 3.0 fusion.158
  39.7 1.9 fusion.156
  42.5 3.0 fusion.158
  46.4 1.9 fusion.156
  49.2 3.1 fusion.158
  53.1 1.9 fusion.156
  56.0 3.1 fusion.158
  59.7 2.6 fusion.118
  66.0 74.3 %scatter_fusion = bf16[8,128,1024]{2,1,0:T(8,128)(2,1)} fusion(bf16[8,128,1024]{2,1,0:T(8,128)(2,1)} %broadcast.162.clone, s32[512]{0:T(512)S(1)} %bitcast.186, bf16[512,1024]{1,0:T(8,128)(2,1)S(1)} %add_convert_fusion.1), kind=kCustom, calls=%fused_computation.3 | custom fusion | bytes 3149824 | tf_op jit(solution)/shard_map/scatter | solution.py:153
  140.4 5.9 all-to-all-start
  147.9 74.2 %scatter_fusion.1 = bf16[8,128,1024]{2,1,0:T(8,128)(2,1)} fusion(bf16[8,128,1024]{2,1,0:T(8,128)(2,1)} %broadcast.162.clone.1, s32[512]{0:T(512)S(1)} %bitcast.187, bf16[512,1024]{1,0:T(8,128)(2,1)S(1)} %copy-done.8), kind=kCustom, calls=%fused_computation.4 | custom fusion | bytes 3149824 | tf_op jit(solution)/shard_map/scatter | solution.py:173
  222.1 4.7 all-to-all-start.2
  227.1 16.0 %fusion.73 = f32[8,128,4096]{2,1,0:T(8,128)} fusion(bf16[8,128,1024]{2,1,0:T(8,128)(2,1)} %all-to-all-done, bf16[1,1024,4096]{2,1,0:T(8,128)(2,1)} %param.27), kind=kOutput, calls=%fused_computation.88 | convolution fusion | flops 8589934592 | bytes 27262976 | tf_op jit(solution)/shard_map/scd,df->scf/dot_general | solution.py:158
  243.0 32.9 %all-to-all-done.2 = bf16[8,128,1024]{2,1,0:T(8,128)(2,1)} async-done(((bf16[8,128,1024]{2,1,0:T(8,128)(2,1)}), bf16[8,128,1024]{2,1,0:T(8,128)(2,1)}, u32[]{:S(2)}, u32[]{:S(2)}) %all-to-all-start.2) | async-done | bytes 2097184 | tf_op jit(solution)/shard_map/all_to_all | solution.py:175
  275.9 17.9 %fusion.78 = bf16[1,4096,1024]{2,1,0:T(8,128)(2,1)} fusion(bf16[8,128,1024]{2,1,0:T(8,128)(2,1)} %all-to-all-done.2, f32[8,128,4096]{2,1,0:T(8,128)} %fusion.73), kind=kOutput, calls=%fused_computation.91 | convolution fusion | flops 8631877632 | bytes 27262976 | tf_op jit(solution)/shard_map/scf,scd->fd/dot_general | solution.py:179
  294.3 25.2 %fusion.66 = bf16[8,128,4096]{2,1,0:T(8,128)(2,1)} fusion(f32[8,128,4096]{2,1,0:T(8,128)} %fusion.73, bf16[8,128,1024]{2,1,0:T(8,128)(2,1)} %all-to-all-done.2, bf16[1,4096,1024]{2,1,0:T(8,128)(2,1)} %param.28), kind=kOutput, calls=%fused_computation.78 | convolution fusion | flops 8673820672 | bytes 35651584 | tf_op jit(solution)/shard_map/scd,fd->scf/dot_general | solution.py:182
  319.6 15.3 %fusion.77 = bf16[1,1024,4096]{2,1,0:T(8,128)(2,1)} fusion(bf16[8,128,1024]{2,1,0:T(8,128)(2,1)} %all-to-all-done, bf16[8,128,4096]{2,1,0:T(8,128)(2,1)} %fusion.66), kind=kOutput, calls=%fused_computation.90 | convolution fusion | flops 8594128896 | bytes 18874368 | tf_op jit(solution)/shard_map/scd,scf->df/dot_general | solution.py:186
  334.8 17.4 %fusion.97 = bf16[8,128,1024]{2,1,0:T(8,128)(2,1)} fusion(bf16[1,4096,1024]{2,1,0:T(8,128)(2,1)} %param.28, f32[8,128,4096]{2,1,0:T(8,128)} %fusion.73), kind=kOutput, calls=%fused_computation.123 | convolution fusion | flops 8628731904 | bytes 27262976 | tf_op jit(solution)/shard_map/scf,fd->scd/dot_general | solution.py:160
  352.3 4.6 all-to-all-start.1
  356.8 15.0 %fusion.94 = bf16[8,128,1024]{2,1,0:T(8,128)(2,1)} fusion(bf16[8,128,4096]{2,1,0:T(8,128)(2,1)} %fusion.66, bf16[1,1024,4096]{2,1,0:T(8,128)(2,1)} %param.27), kind=kOutput, calls=%fused_computation.122 | convolution fusion | flops 8590983168 | bytes 18874368 | tf_op jit(solution)/shard_map/scf,df->scd/dot_general | solution.py:187
  371.8 34.1 %all-to-all-done.1 = bf16[8,128,1024]{2,1,0:T(8,128)(2,1)} async-done(((bf16[8,128,1024]{2,1,0:T(8,128)(2,1)}), bf16[8,128,1024]{2,1,0:T(8,128)(2,1)}, u32[]{:S(2)}, u32[]{:S(2)}) %all-to-all-start.1) | async-done | bytes 2097184 | tf_op jit(solution)/shard_map/all_to_all | solution.py:163
  405.8 4.3 all-to-all-start.3
  410.3 10.7 %gather_fusion.1 = bf16[512,1024]{1,0:T(8,128)(2,1)} fusion(bf16[8,128,1024]{2,1,0:T(8,128)(2,1)} %all-to-all-done.1, s32[512]{0:T(512)S(1)} %bitcast.188), kind=kCustom, calls=%fused_computation.1 | custom fusion | bytes 2101248 | tf_op jit(solution)/shard_map/gather | solution.py:167
  421.0 38.2 %all-to-all-done.3 = bf16[8,128,1024]{2,1,0:T(8,128)(2,1)} async-done(((bf16[8,128,1024]{2,1,0:T(8,128)(2,1)}), bf16[8,128,1024]{2,1,0:T(8,128)(2,1)}, u32[]{:S(2)}, u32[]{:S(2)}) %all-to-all-start.3) | async-done | bytes 2097184 | tf_op jit(solution)/shard_map/all_to_all | solution.py:190
  459.2 8.0 %gather_fusion.2 = bf16[512,1024]{1,0:T(8,128)(2,1)S(1)} fusion(bf16[8,128,1024]{2,1,0:T(8,128)(2,1)} %all-to-all-done.3, s32[512]{0:T(512)S(1)} %bitcast.189), kind=kCustom, calls=%fused_computation.2 | custom fusion | bytes 2101248 | tf_op jit(solution)/shard_map/gather | solution.py:191
  467.3 2.6 fusion.93
  470.0 1.8 fusion.115
  477.1 4.8 fusion.119
  482.6 50.0 %while.29 = (s32[]{:T(128)}, bf16[4,512,4,64]{1,3,2,0:T(8,128)(2,1)}, bf16[4,512,4,64]{1,3,2,0:T(8,128)(2,1)}, bf16[4,512,4,64]{1,3,2,0:T(8,128)(2,1)}, bf16[4,5...) while((s32[]{:T(128)}, ...), condition=%wide.region_19.20_spmd.clone, body=%wide.region_17.19_spmd.clone.sunk | while | flops 687863808 | bytes 65338684 | solution.py:108
  487.0 2.6 multiply_reduce_fusion.3
  499.4 2.6 multiply_reduce_fusion.3
  511.8 2.6 multiply_reduce_fusion.3
  524.2 2.6 multiply_reduce_fusion.3
  532.5 10.2 %fusion.101 = f32[1024,3072]{1,0:T(8,128)} fusion(bf16[512,1024]{0,1:T(8,128)(2,1)} %bitcast.205, bf16[512,1024]{0,1:T(8,128)(2,1)} %bitcast.200, bf16[512,1024]{0,1:T(8,128)(2,1)} %bitcast.202, bf16[512,1024]{1,0:T(8,128)(2,1)S(1)} %copy-done.6, f32[1024]{0:T(1024)S(1)} %copy-done.39, f32[1024]{0:T(1024)S(1)} %copy-done.31, f32[512]{0:T(512)S(1)} %copy-done.25, ...), kind=kOutput, calls=%fused_computation.126 | convolution fusion | flops 3233808384 | bytes 16789504 | tf_op jit(solution)/shard_map/td,te->de/dot_general | solution.py:208
  542.8 7.3 fusion.114
  552.5 37.7 %all-reduce.4 = (f32[1024]{0:T(1024)S(1)}, f32[1024]{0:T(1024)S(1)}, f32[1024]{0:T(1024)S(1)}, f32[1024]{0:T(1024)S(1)}) all-reduce(f32[1024]{0:T(1024)S(1)} %get-tuple-element.147, f32[1024]{0:T(1024)S(1)} %get-tuple-element.151, f32[1024]{0:T(1024)S(1)} %get-tuple-element.149, ...), channel_id=4, replica_groups=mesh['rep'=4,'ep'=8] {'rep','ep'}, use_global_device_ids=true, to_apply=%region_25.26.clone | all-reduce | flops 4096 | bytes 32768
  592.5 4.8 add_add_fusion.2
  597.3 4.1 convert_element_type.109
  601.4 4.1 convert_element_type.106
  605.5 18.8 %reduce-scatter.7.cloned.1.call-done = f32[32,1024]{1,0:T(8,128)} async-done(((f32[1024,1024]{1,0:T(8,128)}), f32[32,1024]{1,0:T(8,128)}) %reduce-scatter.7.cloned.1.call-update) | async-done | bytes 131088 | tf_op jit(solution)/shard_map/reduce_scatter | solution.py:226
  624.3 158.1 %reduce-scatter.5.cloned.1.call-done = f32[32,3072]{1,0:T(8,128)} async-done(((f32[1024,3072]{1,0:T(8,128)}), f32[32,3072]{1,0:T(8,128)}) %reduce-scatter.5.cloned.1.call-update) | async-done | bytes 393232 | tf_op jit(solution)/shard_map/reduce_scatter | solution.py:225
  (217 shorter events, 70.9 us)
Async XLA Ops:
  7.2 52.5 %copy-start = (bf16[1024,1024]{1,0:T(8,128)(2,1)S(1)}, bf16[1024,1024]{1,0:T(8,128)(2,1)}, u32[]{:S(2)}) copy-start(bf16[1024,1024]{1,0:T(8,128)(2,1)} %param.24) | copy-start | bytes 6291460
  7.2 8.7 %copy-start.32 = (s32[512]{0:T(512)S(1)}, s32[512]{0:T(512)}, u32[]{:S(2)}) copy-start(s32[512]{0:T(512)} %param.18) | copy-start | bytes 6148
  7.2 10.2 %copy-start.5 = (bf16[512,1024]{1,0:T(8,128)(2,1)S(1)}, bf16[512,1024]{1,0:T(8,128)(2,1)}, u32[]{:S(2)}) copy-start(bf16[512,1024]{1,0:T(8,128)(2,1)} %param.17) | copy-start | bytes 3145732
  7.2 5.5 copy-start.2
  7.2 10.2 %copy-start.30 = (f32[1024]{0:T(1024)S(1)}, f32[1024]{0:T(1024)}, u32[]{:S(2)}) copy-start(f32[1024]{0:T(1024)} %param.21) | copy-start | bytes 12292
  7.2 10.2 %copy-start.38 = (f32[1024]{0:T(1024)S(1)}, f32[1024]{0:T(1024)}, u32[]{:S(2)}) copy-start(f32[1024]{0:T(1024)} %param.22) | copy-start | bytes 12292
  10.5 13.7 %copy-start.20 = (f32[512]{0:T(512)}, f32[512]{0:T(512)S(1)}, u32[]{:S(2)}) copy-start(f32[512]{0:T(512)S(1)} %broadcast_multiply_fusion.1) | copy-start | bytes 6148
  12.7 11.4 %copy-start.24 = (f32[512]{0:T(512)}, f32[512]{0:T(512)S(1)}, u32[]{:S(2)}) copy-start(f32[512]{0:T(512)S(1)} %fusion.107) | copy-start | bytes 6148
  59.6 4.4 copy-start.18
  59.6 4.4 copy-start.33
  140.4 7.5 copy-start.8
  140.4 81.7 %all-to-all-start = ((bf16[8,128,1024]{2,1,0:T(8,128)(2,1)}), bf16[8,128,1024]{2,1,0:T(8,128)(2,1)}, u32[]{:S(2)}, u32[]{:S(2)}) async-start(bf16[8,128,1024]{2,1,0:T(8,128)(2,1)} %scatter_fusion), calls=%async_computation | async-start | bytes 4194304 | tf_op jit(solution)/shard_map/all_to_all | solution.py:157
  222.1 53.8 %all-to-all-start.2 = ((bf16[8,128,1024]{2,1,0:T(8,128)(2,1)}), bf16[8,128,1024]{2,1,0:T(8,128)(2,1)}, u32[]{:S(2)}, u32[]{:S(2)}) async-start(bf16[8,128,1024]{2,1,0:T(8,128)(2,1)} %scatter_fusion.1), calls=%async_computation.2 | async-start | bytes 4194304 | tf_op jit(solution)/shard_map/all_to_all | solution.py:175
  226.8 370.5 %reduce-scatter.11.cloned.1.call-start = ((), (), s32[]{:S(2)}) async-start(), calls=%async_computation.11 | async-start | bytes 10485760 | tf_op jit(solution)/shard_map/reduce_scatter | solution.py:220
  293.9 307.5 %reduce-scatter.9.cloned.1.call-start = ((), (), s32[]{:S(2)}) async-start(), calls=%async_computation.10 | async-start | bytes 10485760 | tf_op jit(solution)/shard_map/reduce_scatter | solution.py:217
  352.3 53.6 %all-to-all-start.1 = ((bf16[8,128,1024]{2,1,0:T(8,128)(2,1)}), bf16[8,128,1024]{2,1,0:T(8,128)(2,1)}, u32[]{:S(2)}, u32[]{:S(2)}) async-start(bf16[8,128,1024]{2,1,0:T(8,128)(2,1)} %fusion.97), calls=%async_computation.1 | async-start | bytes 4194304 | tf_op jit(solution)/shard_map/all_to_all | solution.py:163
  371.8 38.5 %copy-start.1 = (s32[512,1]{0,1:T(1,128)S(1)}, s32[512,1]{0,1:T(1,128)}, u32[]{:S(2)}) copy-start(s32[512,1]{0,1:T(1,128)} %get-tuple-element.195) | copy-start | bytes 6148
  405.8 53.4 %all-to-all-start.3 = ((bf16[8,128,1024]{2,1,0:T(8,128)(2,1)}), bf16[8,128,1024]{2,1,0:T(8,128)(2,1)}, u32[]{:S(2)}, u32[]{:S(2)}) async-start(bf16[8,128,1024]{2,1,0:T(8,128)(2,1)} %fusion.94), calls=%async_computation.3 | async-start | bytes 4194304 | tf_op jit(solution)/shard_map/all_to_all | solution.py:190
  410.2 214.1 %reduce-scatter.7.cloned.1.call-start = ((), (), s32[]{:S(2)}) async-start(), calls=%async_computation.9 | async-start | bytes 4325376 | tf_op jit(solution)/shard_map/reduce_scatter | solution.py:226
  421.0 46.3 %copy-start.17 = (f32[512]{0:T(512)S(1)}, f32[512]{0:T(512)}, u32[]{:S(2)}) copy-start(f32[512]{0:T(512)} %copy-done.16) | copy-start | bytes 6148
  421.0 46.3 %copy-start.19 = (f32[1024]{0:T(1024)S(1)}, f32[1024]{0:T(1024)}, u32[]{:S(2)}) copy-start(f32[1024]{0:T(1024)} %param.25) | copy-start | bytes 12292
  421.0 46.3 %copy-start.23 = (f32[512]{0:T(512)S(1)}, f32[512]{0:T(512)}, u32[]{:S(2)}) copy-start(f32[512]{0:T(512)} %copy-done.22) | copy-start | bytes 6148
  467.3 2.7 copy-start.29
  467.3 2.7 copy-start.4
  467.3 2.7 copy-start.12
  470.0 3.2 copy-start.9
  481.9 300.5 %reduce-scatter.5.cloned.1.call-start = ((), (), s32[]{:S(2)}) async-start(), calls=%async_computation.8 | async-start | bytes 12976128 | tf_op jit(solution)/shard_map/reduce_scatter | solution.py:225
  482.5 50.0 %copy-start.6 = (bf16[512,1024]{1,0:T(8,128)(2,1)S(1)}, bf16[512,1024]{1,0:T(8,128)(2,1)}, u32[]{:S(2)}) copy-start(bf16[512,1024]{1,0:T(8,128)(2,1)} %param.17) | copy-start | bytes 3145732
  482.5 50.0 %copy-start.21 = (f32[512]{0:T(512)S(1)}, f32[512]{0:T(512)}, u32[]{:S(2)}) copy-start(f32[512]{0:T(512)} %copy-done.20) | copy-start | bytes 6148
  482.5 50.0 %copy-start.25 = (f32[512]{0:T(512)S(1)}, f32[512]{0:T(512)}, u32[]{:S(2)}) copy-start(f32[512]{0:T(512)} %copy-done.24) | copy-start | bytes 6148
  482.5 50.0 %copy-start.31 = (f32[1024]{0:T(1024)S(1)}, f32[1024]{0:T(1024)}, u32[]{:S(2)}) copy-start(f32[1024]{0:T(1024)} %param.21) | copy-start | bytes 12292
  482.5 50.0 %copy-start.39 = (f32[1024]{0:T(1024)S(1)}, f32[1024]{0:T(1024)}, u32[]{:S(2)}) copy-start(f32[1024]{0:T(1024)} %param.22) | copy-start | bytes 12292
  482.8 2.9 copy-start.11
  482.8 2.9 copy-start.40
  487.0 2.7 copy-start.41
  489.6 3.0 copy-start.36
  495.3 2.9 copy-start.11
  495.3 2.9 copy-start.40
  502.0 3.0 copy-start.36
  507.7 2.9 copy-start.11
  507.7 2.9 copy-start.40
  511.8 2.7 copy-start.41
  514.5 3.0 copy-start.36
  520.1 2.9 copy-start.11
  520.1 2.9 copy-start.40
  524.2 2.7 copy-start.41
  526.9 3.0 copy-start.36
  542.8 7.4 copy-start.27
  (23 other events, 32.2 us)
Sparse Core Ops, SparseCore 0:
  294.0 84.7 reduce-scatter.10
  381.8 86.3 reduce-scatter.8
  482.0 142.2 reduce-scatter.6
  630.7 151.6 reduce-scatter.4
where the time goes:
time: 804 us; the launch traced here: 789 us
  waiting for transfers between devices  282 us (35%)
  local copies, waits for them, and re-layouts  199 us (25%)
  matrix products  196 us (24%)
  other arithmetic  39 us (5%)
  blocking collectives  37.7 us (5%)
  starting transfers between devices  20.3 us (3%)
  between operations  14.8 us (2%)
    reduce_scatter x1, waiting for transfers between devices, local(): lax.psum_scatter(grad_project_in, ('rep', 'ep'), scatter_dimension=0, til...  158 us
    scatter x1, local copies, waits for them, and re-layouts, local(): dispatch_buffer = jnp.zeros((expert_count, capacity, model_width), jnp.bf...  74.3 us
    scatter x1, local copies, waits for them, and re-layouts, local(): grad_buffer = jnp.zeros((expert_count, capacity, model_width), jnp.bfloat...  74.2 us
    all_to_all x1, waiting for transfers between devices, local(): lax.all_to_all(grad_routed, 'ep', split_axis=0, concat_axis=0, tiled=True)  38.2 us
    unnamed x1, blocking collectives  37.7 us
    all_to_all x1, waiting for transfers between devices, local(): lax.all_to_all(result, 'ep', split_axis=0, concat_axis=0, tiled=True)  34.1 us
    all_to_all x1, waiting for transfers between devices, local(): lax.all_to_all(grad_buffer, 'ep', split_axis=0, concat_axis=0, tiled=True)  32.9 us
    dot_general x1, matrix products, local(): jnp.einsum('scd,fd->scf', grad_received, second_weight, preferred_element...  25.2 us
  transfers between devices with their start and end apart: 8, of which 5 were waited for; matrix products, arithmetic and copies ran while one was open for 35% of the time, Pallas kernels for 0%

commit v1 on v0

--- a/solution.py
+++ b/solution.py
@@ -106,6 +106,21 @@
         return (grad_query, grad_key, grad_value)
 
     return lax.map(head_group, (query_heads, key_heads, value_heads, grad_heads, log_totals))
+
+
+def gather_slots(slot_hot, buffer):
+    rows = buffer.reshape(-1, buffer.shape[-1])
+    return jnp.einsum("st,sd->td", slot_hot, rows, preferred_element_type=jnp.float32)
+
+
+def scatter_sum(parts):
+    rep_size, ep_size = lax.axis_size("rep"), lax.axis_size("ep")
+    rows, width = parts.shape
+    tile = rows // (rep_size * ep_size)
+    parts = jnp.swapaxes(parts.reshape(rep_size, ep_size, tile, width), 0, 1)
+    parts = parts.reshape(rows, width)
+    parts = lax.psum_scatter(parts, "ep", scatter_dimension=0, tiled=True)
+    return lax.psum_scatter(parts, "rep", scatter_dimension=0, tiled=True)
 
 
 def local(
@@ -129,6 +144,18 @@
     expert_count = expert_in.shape[0] * lax.axis_size("ep")
     capacity = 2 * tok_rows // expert_count
     inputs = tokens_in.astype(jnp.float32)
+    expert_ids = jnp.take(hash_table, token_ids)
+    slot_rank = slot_ranks(expert_ids, expert_count)
+    slot_of = expert_ids * capacity + slot_rank
+    slot_hot = (
+        jnp.arange(expert_count * capacity, dtype=jnp.int32)[:, None] == slot_of[None, :]
+    ).astype(jnp.bfloat16)
+    grad_buffer = (
+        jnp.dot(slot_hot, out_grad, preferred_element_type=jnp.float32)
+        .astype(jnp.bfloat16)
+        .reshape(expert_count, capacity, model_width)
+    )
+    grad_received = lax.all_to_all(grad_buffer, "ep", split_axis=0, concat_axis=0, tiled=True)
     attend_mask = document_mask(doc_lengths[0], tok_rows)
     normed_one, pull_one = jax.vjp(layer_norm, inputs, gain_one, shift_one)
     normed_one_low = normed_one.astype(jnp.bfloat16)
@@ -145,34 +172,12 @@
     hidden = inputs + jnp.dot(mixture, project_out, preferred_element_type=jnp.float32)
     normed_two, pull_two = jax.vjp(layer_norm, hidden, gain_two, shift_two)
     routed = normed_two.astype(jnp.bfloat16)
-    expert_ids = jnp.take(hash_table, token_ids)
-    slot_rank = slot_ranks(expert_ids, expert_count)
-    dispatch_buffer = (
-        jnp.zeros((expert_count, capacity, model_width), jnp.bfloat16)
-        .at[expert_ids, slot_rank]
-        .set(routed)
-    )
+    dispatch_buffer = jnp.dot(
+        slot_hot, routed, preferred_element_type=jnp.float32
+    ).astype(jnp.bfloat16).reshape(expert_count, capacity, model_width)
     first_weight = expert_in[0]
     second_weight = expert_out[0]
     received = lax.all_to_all(dispatch_buffer, "ep", split_axis=0, concat_axis=0, tiled=True)
-    pre_act = jnp.einsum("scd,df->scf", received, first_weight, preferred_element_type=jnp.float32)
-    activation = smooth_gate(pre_act).astype(jnp.bfloat16)
-    result = jnp.einsum(
-        "scf,fd->scd", activation, second_weight, preferred_element_type=jnp.float32
-    ).astype(jnp.bfloat16)
-    returned = lax.all_to_all(result, "ep", split_axis=0, concat_axis=0, tiled=True)
-    outcome = (returned, received)
-    returned = outcome[0]
-    received = outcome[1]
-    block_sum = hidden + returned[expert_ids, slot_rank].astype(jnp.float32)
-    block_out = block_sum.astype(jnp.bfloat16)
-    grad_out = out_grad.astype(jnp.float32)
-    grad_buffer = (
-        jnp.zeros((expert_count, capacity, model_width), jnp.bfloat16)
-        .at[expert_ids, slot_rank]
-        .set(out_grad)
-    )
-    grad_received = lax.all_to_all(grad_buffer, "ep", split_axis=0, concat_axis=0, tiled=True)
     pre_act = jnp.einsum("scd,df->scf", received, first_weight, preferred_element_type=jnp.float32)
     gate_value, gate_pull = jax.vjp(smooth_gate, pre_act)
     activation = gate_value.astype(jnp.bfloat16)
@@ -188,7 +193,13 @@
         "scf,df->scd", grad_pre, first_weight, preferred_element_type=jnp.float32
     ).astype(jnp.bfloat16)
     grad_back = lax.all_to_all(grad_routed, "ep", split_axis=0, concat_axis=0, tiled=True)
-    grad_normed_two = grad_back[expert_ids, slot_rank].astype(jnp.float32)
+    result = jnp.einsum(
+        "scf,fd->scd", activation, second_weight, preferred_element_type=jnp.float32
+    ).astype(jnp.bfloat16)
+    returned = lax.all_to_all(result, "ep", split_axis=0, concat_axis=0, tiled=True)
+    block_out = (hidden + gather_slots(slot_hot, returned)).astype(jnp.bfloat16)
+    grad_out = out_grad.astype(jnp.float32)
+    grad_normed_two = gather_slots(slot_hot, grad_back)
     hidden_part, grad_gain_two, grad_shift_two = pull_two(grad_normed_two)
     grad_hidden = grad_out + hidden_part
     grad_hidden_low = grad_hidden.astype(jnp.bfloat16)
@@ -221,23 +232,21 @@
             grad_second[None].astype(jnp.bfloat16), "rep", scatter_dimension=1, tiled=True
         ).astype(jnp.float32),
     )
-    dense_parts = (
-        lax.psum_scatter(grad_project_in, ("rep", "ep"), scatter_dimension=0, tiled=True),
-        lax.psum_scatter(grad_project_out, ("rep", "ep"), scatter_dimension=0, tiled=True),
-        lax.psum_scatter(grad_gain_one, ("rep", "ep"), scatter_dimension=0, tiled=True),
-        lax.psum_scatter(grad_shift_one, ("rep", "ep"), scatter_dimension=0, tiled=True),
-        lax.psum_scatter(grad_gain_two, ("rep", "ep"), scatter_dimension=0, tiled=True),
-        lax.psum_scatter(grad_shift_two, ("rep", "ep"), scatter_dimension=0, tiled=True),
-    )
+    small = jnp.stack([grad_gain_one, grad_shift_one, grad_gain_two, grad_shift_two], 1)
+    small = jnp.pad(small, ((0, 0), (0, 124))).astype(jnp.bfloat16)
+    dense = jnp.concatenate(
+        [grad_project_in.astype(jnp.bfloat16), grad_project_out.astype(jnp.bfloat16), small], 1
+    )
+    summed = scatter_sum(dense).astype(jnp.float32)
     return (
         block_out,
         grad_in,
-        dense_parts[0],
-        dense_parts[1],
-        dense_parts[2],
-        dense_parts[3],
-        dense_parts[4],
-        dense_parts[5],
+        summed[:, : 3 * model_width],
+        summed[:, 3 * model_width : 4 * model_width],
+        summed[:, 4 * model_width],
+        summed[:, 4 * model_width + 1],
+        summed[:, 4 * model_width + 2],
+        summed[:, 4 * model_width + 3],
         summed_first,
         summed_second,
     )

time: 804 us -> 721 us (0.90)
  local copies, waits for them, and re-layouts: 199 us -> 34.8 us
  waiting for transfers between devices: 282 us -> 401 us
  blocking collectives: 37.7 us -> 0 us
    scatter x2 -> x0, local copies, waits for them, and re-layouts: 149 us -> none  [the longest x1 74.3 us: local(): dispatch_buffer = jnp.zeros((expert_count, capacity, model_width), jnp.bf...]
    reduce_scatter x1, waiting for transfers between devices: 0.01 us -> 85.2 us  [local(): lax.psum_scatter(grad_first[None].astype(jnp.bfloat16), 'rep', scatter_di...]
    reduce_scatter x1, waiting for transfers between devices: 0.01 us -> 84.5 us  [local(): lax.psum_scatter(grad_second[None].astype(jnp.bfloat16), 'rep', scatter_d...]
    reduce_scatter x2, waiting for transfers between devices: 177 us -> 93.7 us  [the longest x1 66.8 us: scatter_sum(): parts = lax.psum_scatter(parts, 'ep', scatter_dimension=0, tiled=True)]
    all_to_all x1, waiting for transfers between devices: 0.01 us -> 46.6 us  [local(): lax.all_to_all(dispatch_buffer, 'ep', split_axis=0, concat_axis=0, tiled=...]
    unnamed x1 -> x0, blocking collectives: 37.7 us -> none
    all_to_all x1, waiting for transfers between devices: 34.1 us -> 9.18 us  [local(): lax.all_to_all(result, 'ep', split_axis=0, concat_axis=0, tiled=True)]
    gather x2 -> x0, local copies, waits for them, and re-layouts: 18.7 us -> none  [the longest x1 10.7 us: local(): block_sum = hidden + returned[expert_ids, slot_rank].astype(jnp.float32)]
  transfers between devices with their start and end apart: 8 -> 8, of which waited for: 5 -> 8; matrix products, arithmetic and copies ran while one was open for 35% -> 12% of each run, Pallas kernels for 0% -> 0%
where the time goes in v1:
time: 721 us; the launch traced here: 711 us
  waiting for transfers between devices  401 us (56%)
  matrix products  202 us (28%)
  other arithmetic  38.4 us (5%)
  local copies, waits for them, and re-layouts  34.8 us (5%)
  starting transfers between devices  19.2 us (3%)
  between operations  14.8 us (2%)
    reduce_scatter x1, waiting for transfers between devices, local(): lax.psum_scatter(grad_first[None].astype(jnp.bfloat16), 'rep', scatter_di...  85.2 us
    reduce_scatter x1, waiting for transfers between devices, local(): lax.psum_scatter(grad_second[None].astype(jnp.bfloat16), 'rep', scatter_d...  84.5 us
    reduce_scatter x1, waiting for transfers between devices, scatter_sum(): parts = lax.psum_scatter(parts, 'ep', scatter_dimension=0, tiled=True)  66.8 us
    all_to_all x1, waiting for transfers between devices, local(): lax.all_to_all(grad_routed, 'ep', split_axis=0, concat_axis=0, tiled=True)  49 us
    all_to_all x1, waiting for transfers between devices, local(): lax.all_to_all(dispatch_buffer, 'ep', split_axis=0, concat_axis=0, tiled=...  46.6 us
    all_to_all x1, waiting for transfers between devices, local(): lax.all_to_all(grad_buffer, 'ep', split_axis=0, concat_axis=0, tiled=True)  33.1 us
    reduce_scatter x1, waiting for transfers between devices, scatter_sum(): return lax.psum_scatter(parts, 'rep', scatter_dimension=0, tiled=True)  26.9 us
    dot_general x1, matrix products, local(): jnp.einsum('scd,fd->scf', grad_received, second_weight, preferred_element...  24.7 us
  transfers between devices with their start and end apart: 8, of which 8 were waited for; matrix products, arithmetic and copies ran while one was open for 12% of the time, Pallas kernels for 0%

profile of v1, /device:TPU:0, one launch (start us, length us, event | category | flops | bytes accessed | tf_op | source)
XLA Modules:
  0.0 711.0 jit_solution(11951787239231415054)
XLA Ops:
  9.0 3.4 gather_fusion
  18.4 6.7 convolution_convert_fusion.1
  26.8 2.3 copy.70
  29.1 2.3 copy.69
  31.4 2.3 copy.68
  33.7 24.5 %while.28 = (s32[]{:T(128)}, bf16[4,512,4,64]{1,3,2,0:T(8,128)(2,1)}, f32[4,4,512]{2,1,0:T(4,128)S(1)}, bf16[4,512,4,64]{1,3,2,0:T(8,128)(2,1)}, bf16[4,512,4,64...) while((s32[]{:T(128)}, ...), condition=%wide.region_7.8_spmd.clone, body=%wide.region_4.7_spmd.clone.sunk | while | flops 281933824 | bytes 14749793 | solution.py:75
  36.7 3.0 fusion.168
  42.9 3.0 fusion.168
  49.0 3.0 fusion.168
  55.1 3.0 fusion.168
  58.2 2.6 fusion.126
  61.2 2.8 fusion.102
  64.0 6.3 all-to-all-start
  70.4 2.6 fusion.103
  73.0 46.6 %all-to-all-done = bf16[8,128,1024]{2,1,0:T(8,128)(2,1)} async-done(((bf16[8,128,1024]{2,1,0:T(8,128)(2,1)}), bf16[8,128,1024]{2,1,0:T(8,128)(2,1)}, u32[]{:S(2)}, u32[]{:S(2)}) %all-to-all-start) | async-done | bytes 2097184 | tf_op jit(solution)/shard_map/all_to_all | solution.py:180
  119.5 4.6 all-to-all-start.2
  124.1 16.0 %fusion.75 = f32[8,128,4096]{2,1,0:T(8,128)} fusion(bf16[8,128,1024]{2,1,0:T(8,128)(2,1)} %all-to-all-done, bf16[1,1024,4096]{2,1,0:T(8,128)(2,1)} %param.27), kind=kOutput, calls=%fused_computation.87 | convolution fusion | flops 8589934592 | bytes 27262976 | tf_op jit(solution)/shard_map/scd,df->scf/dot_general | solution.py:181
  140.1 33.1 %all-to-all-done.2 = bf16[8,128,1024]{2,1,0:T(8,128)(2,1)} async-done(((bf16[8,128,1024]{2,1,0:T(8,128)(2,1)}), bf16[8,128,1024]{2,1,0:T(8,128)(2,1)}, u32[]{:S(2)}, u32[]{:S(2)}) %all-to-all-start.2) | async-done | bytes 2097184 | tf_op jit(solution)/shard_map/all_to_all | solution.py:158
  173.2 24.7 %fusion.67 = bf16[8,128,4096]{2,1,0:T(8,128)(2,1)} fusion(f32[8,128,4096]{2,1,0:T(8,128)} %fusion.75, bf16[8,128,1024]{2,1,0:T(8,128)(2,1)} %all-to-all-done.2, bf16[1,4096,1024]{2,1,0:T(8,128)(2,1)} %param.28), kind=kOutput, calls=%fused_computation.76 | convolution fusion | flops 8673820672 | bytes 35651584 | tf_op jit(solution)/shard_map/scd,fd->scf/dot_general | solution.py:187
  197.9 15.1 %fusion.96 = bf16[8,128,1024]{2,1,0:T(8,128)(2,1)} fusion(bf16[8,128,4096]{2,1,0:T(8,128)(2,1)} %fusion.67, bf16[1,1024,4096]{2,1,0:T(8,128)(2,1)} %param.27), kind=kOutput, calls=%fused_computation.122 | convolution fusion | flops 8590983168 | bytes 18874368 | tf_op jit(solution)/shard_map/scf,df->scd/dot_general | solution.py:192
  213.0 4.3 all-to-all-start.3
  217.5 49.0 %all-to-all-done.3 = bf16[8,128,1024]{2,1,0:T(8,128)(2,1)} async-done(((bf16[8,128,1024]{2,1,0:T(8,128)(2,1)}), bf16[8,128,1024]{2,1,0:T(8,128)(2,1)}, u32[]{:S(2)}, u32[]{:S(2)}) %all-to-all-start.3) | async-done | bytes 2097184 | tf_op jit(solution)/shard_map/all_to_all | solution.py:195
  266.4 4.1 multiply_reduce_fusion.1
  271.8 2.6 convolution_convert_fusion.2
  274.4 2.3 convolution_convert_fusion.3
  276.6 2.4 copy.71
  279.1 44.1 %while.29 = (s32[]{:T(128)}, bf16[4,512,4,64]{1,3,2,0:T(8,128)(2,1)}, bf16[4,512,4,64]{1,3,2,0:T(8,128)(2,1)}, bf16[4,512,4,64]{1,3,2,0:T(8,128)(2,1)}, bf16[4,5...) while((s32[]{:T(128)}, ...), condition=%wide.region_17.18_spmd.clone, body=%wide.region_15.17_spmd.clone.sunk | while | flops 687863808 | bytes 65338684 | solution.py:108
  282.5 2.6 multiply_reduce_fusion.5
  293.5 2.7 multiply_reduce_fusion.5
  304.5 2.6 multiply_reduce_fusion.5
  315.5 2.6 multiply_reduce_fusion.5
  323.3 7.4 %fusion.91 = (f32[512]{0:T(512)S(1)}, f32[512,1024]{1,0:T(8,128)S(1)}) fusion(bf16[512,1024]{1,0:T(8,128)(2,1)S(1)} %copy-done.3, f32[1024]{0:T(1024)S(1)} %copy-done.25, f32[512]{0:T(512)S(1)} %copy-done.17, bf16[1024,3072]{1,0:T(8,128)(2,1)} %param.23, bf16[512,1024]{0,1:T(8,128)(2,1)} %bitcast.209, bf16[512,1024]{0,1:T(8,128)(2,1)} %bitcast.204, ...), kind=kOutput, calls=%fused_computation.109 | convolution fusion | flops 3233283584 | bytes 12591104 | tf_op jit(solution)/shard_map/te,de->td/dot_general | solution.py:222
  330.7 8.9 %convolution_convert_fusion = bf16[1024,3072]{1,0:T(8,128)(2,1)} fusion(bf16[512,1024]{0,1:T(8,128)(2,1)S(1)} %bitcast.210, bf16[512,1024]{0,1:T(8,128)(2,1)S(1)} %bitcast.205, bf16[512,1024]{0,1:T(8,128)(2,1)S(1)} %bitcast.207, bf16[512,1024]{1,0:T(8,128)(2,1)S(1)} %copy-done.3, f32[1024]{0:T(1024)S(1)} %copy-done.37, f32[1024]{0:T(1024)S(1)} %copy-done.25, ...), kind=kOutput, calls=%fused_computation.91 | convolution fusion | flops 3236954112 | bytes 10498048 | tf_op jit(solution)/shard_map/td,te->de/dot_general | solution.py:219
  341.0 7.1 %fusion.68 = bf16[1024,4224]{1,0:T(8,128)(2,1)} fusion(bf16[1024,4]{1,0:T(8,128)(2,1)S(1)} %copy.73, bf16[1024,1024]{1,0:T(8,128)(2,1)} %convolution_convert_fusion.2, bf16[1024,3072]{1,0:T(8,128)(2,1)} %convolution_convert_fusion), kind=kLoop, calls=%fused_computation.80 | loop fusion | flops 34603008 | bytes 17047552 | tf_op jit(solution)/shard_map/concatenate | solution.py:237
  348.1 7.7 %copy.74 = bf16[8,4,32,4224]{3,2,1,0:T(8,128)(2,1)} copy(bf16[8,4,32,4224]{3,2,0,1:T(8,128)(2,1)} %bitcast.192) | data formatting | bytes 17301504 | tf_op jit(solution)/shard_map/transpose | solution.py:120
  355.9 17.9 %fusion.80 = bf16[1,4096,1024]{2,1,0:T(8,128)(2,1)} fusion(bf16[8,128,1024]{2,1,0:T(8,128)(2,1)} %all-to-all-done.2, f32[8,128,4096]{2,1,0:T(8,128)} %fusion.75), kind=kOutput, calls=%fused_computation.90 | convolution fusion | flops 8631877632 | bytes 27262976 | tf_op jit(solution)/shard_map/scf,scd->fd/dot_general | solution.py:184
  373.9 15.2 %fusion.79 = bf16[1,1024,4096]{2,1,0:T(8,128)(2,1)} fusion(bf16[8,128,1024]{2,1,0:T(8,128)(2,1)} %all-to-all-done, bf16[8,128,4096]{2,1,0:T(8,128)(2,1)} %fusion.67), kind=kOutput, calls=%fused_computation.89 | convolution fusion | flops 8594128896 | bytes 18874368 | tf_op jit(solution)/shard_map/scd,scf->df/dot_general | solution.py:191
  389.1 17.2 %fusion.99 = bf16[8,128,1024]{2,1,0:T(8,128)(2,1)} fusion(bf16[1,4096,1024]{2,1,0:T(8,128)(2,1)} %param.28, f32[8,128,4096]{2,1,0:T(8,128)} %fusion.75), kind=kOutput, calls=%fused_computation.123 | convolution fusion | flops 8628731904 | bytes 27262976 | tf_op jit(solution)/shard_map/scf,fd->scd/dot_general | solution.py:196
  406.2 3.7 all-to-all-start.1
  410.0 66.8 %reduce-scatter.5.cloned.1.call-done = bf16[128,4224]{1,0:T(8,128)(2,1)} async-done(((bf16[1024,4224]{1,0:T(8,128)(2,1)}), bf16[128,4224]{1,0:T(8,128)(2,1)}) %reduce-scatter.5.cloned.1.call-update) | async-done | bytes 1081360 | tf_op jit(solution)/shard_map/reduce_scatter | solution.py:122
  476.9 9.2 %all-to-all-done.1 = bf16[8,128,1024]{2,1,0:T(8,128)(2,1)S(1)} async-done(((bf16[8,128,1024]{2,1,0:T(8,128)(2,1)}), bf16[8,128,1024]{2,1,0:T(8,128)(2,1)S(1)}, u32[]{:S(2)}, u32[]{:S(2)}) %all-to-all-start.1) | async-done | bytes 2097184 | tf_op jit(solution)/shard_map/all_to_all | solution.py:199
  487.4 4.6 add_convert_fusion
  492.1 2.2 add_add_fusion.2
  494.3 84.5 %reduce-scatter.11.cloned.1.call-done = bf16[1,1024,1024]{2,1,0:T(8,128)(2,1)} async-done(((bf16[1,4096,1024]{2,1,0:T(8,128)(2,1)}), bf16[1,1024,1024]{2,1,0:T(8,128)(2,1)}) %reduce-scatter.11.cloned.1.call-update) | async-done | bytes 2097168 | tf_op jit(solution)/shard_map/reduce_scatter | solution.py:231
  578.8 4.2 convert_element_type.124
  583.0 85.2 %reduce-scatter.9.cloned.1.call-done = bf16[1,256,4096]{2,1,0:T(8,128)(2,1)} async-done(((bf16[1,1024,4096]{2,1,0:T(8,128)(2,1)}), bf16[1,256,4096]{2,1,0:T(8,128)(2,1)}) %reduce-scatter.9.cloned.1.call-update) | async-done | bytes 2097168 | tf_op jit(solution)/shard_map/reduce_scatter | solution.py:228
  668.2 4.1 convert_element_type.121
  672.3 26.9 %reduce-scatter.7.cloned.1.call-done = bf16[32,4224]{1,0:T(8,128)(2,1)} async-done(((bf16[128,4224]{1,0:T(8,128)(2,1)}), bf16[32,4224]{1,0:T(8,128)(2,1)}) %reduce-scatter.7.cloned.1.call-update) | async-done | bytes 270352 | tf_op jit(solution)/shard_map/reduce_scatter | solution.py:123
  (218 shorter events, 64.1 us)
Async XLA Ops:
  7.2 51.0 %copy-start = (bf16[1024,1024]{1,0:T(8,128)(2,1)S(1)}, bf16[1024,1024]{1,0:T(8,128)(2,1)}, u32[]{:S(2)}) copy-start(bf16[1024,1024]{1,0:T(8,128)(2,1)} %param.24) | copy-start | bytes 6291460
  7.2 11.1 %copy-start.2 = (bf16[512,1024]{1,0:T(8,128)(2,1)S(1)}, bf16[512,1024]{1,0:T(8,128)(2,1)}, u32[]{:S(2)}) copy-start(bf16[512,1024]{1,0:T(8,128)(2,1)} %param.17) | copy-start | bytes 3145732
  7.2 11.1 %copy-start.24 = (f32[1024]{0:T(1024)S(1)}, f32[1024]{0:T(1024)}, u32[]{:S(2)}) copy-start(f32[1024]{0:T(1024)} %param.21) | copy-start | bytes 12292
  7.2 11.1 %copy-start.36 = (f32[1024]{0:T(1024)S(1)}, f32[1024]{0:T(1024)}, u32[]{:S(2)}) copy-start(f32[1024]{0:T(1024)} %param.22) | copy-start | bytes 12292
  14.6 10.5 %copy-start.16 = (f32[512]{0:T(512)}, f32[512]{0:T(512)S(1)}, u32[]{:S(2)}) copy-start(f32[512]{0:T(512)S(1)} %broadcast_multiply_fusion.1) | copy-start | bytes 6148
  16.2 8.8 %copy-start.18 = (f32[512]{0:T(512)}, f32[512]{0:T(512)S(1)}, u32[]{:S(2)}) copy-start(f32[512]{0:T(512)S(1)} %fusion.117) | copy-start | bytes 6148
  18.3 248.1 %copy-start.27 = (s32[512]{0:T(512)}, s32[512]{0:T(512)S(1)}, u32[]{:S(2)}) copy-start(s32[512]{0:T(512)S(1)} %multiply_add_fusion.1) | copy-start | bytes 6148
  58.2 3.0 copy-start.26
  58.2 3.0 copy-start.35
  60.8 3.2 copy-start.7
  61.2 9.2 %copy-start.12 = (bf16[512,1024]{1,0:T(8,128)(2,1)S(1)}, bf16[512,1024]{1,0:T(8,128)(2,1)}, u32[]{:S(2)}) copy-start(bf16[512,1024]{1,0:T(8,128)(2,1)} %param.29) | copy-start | bytes 3145732
  64.0 55.5 %all-to-all-start = ((bf16[8,128,1024]{2,1,0:T(8,128)(2,1)}), bf16[8,128,1024]{2,1,0:T(8,128)(2,1)}, u32[]{:S(2)}, u32[]{:S(2)}) async-start(bf16[8,128,1024]{2,1,0:T(8,128)(2,1)} %bitcast.199), calls=%async_computation | async-start | bytes 4194304 | tf_op jit(solution)/shard_map/all_to_all | solution.py:180
  119.5 53.6 %all-to-all-start.2 = ((bf16[8,128,1024]{2,1,0:T(8,128)(2,1)}), bf16[8,128,1024]{2,1,0:T(8,128)(2,1)}, u32[]{:S(2)}, u32[]{:S(2)}) async-start(bf16[8,128,1024]{2,1,0:T(8,128)(2,1)} %bitcast.198), calls=%async_computation.2 | async-start | bytes 4194304 | tf_op jit(solution)/shard_map/all_to_all | solution.py:158
  213.0 53.4 %all-to-all-start.3 = ((bf16[8,128,1024]{2,1,0:T(8,128)(2,1)}), bf16[8,128,1024]{2,1,0:T(8,128)(2,1)}, u32[]{:S(2)}, u32[]{:S(2)}) async-start(bf16[8,128,1024]{2,1,0:T(8,128)(2,1)} %fusion.96), calls=%async_computation.3 | async-start | bytes 4194304 | tf_op jit(solution)/shard_map/all_to_all | solution.py:195
  217.4 259.5 %reduce-scatter.5.cloned.1.call-start = ((), (), s32[]{:S(2)}) async-start(), calls=%async_computation.8 | async-start | bytes 9732096 | tf_op jit(solution)/shard_map/reduce_scatter | solution.py:122
  266.4 4.1 copy-start.8
  271.3 3.1 copy-start.5
  271.3 3.1 copy-start.20
  274.4 4.7 copy-start.4
  279.1 44.1 %copy-start.3 = (bf16[512,1024]{1,0:T(8,128)(2,1)S(1)}, bf16[512,1024]{1,0:T(8,128)(2,1)}, u32[]{:S(2)}) copy-start(bf16[512,1024]{1,0:T(8,128)(2,1)} %param.17) | copy-start | bytes 3145732
  279.1 44.1 %copy-start.17 = (f32[512]{0:T(512)S(1)}, f32[512]{0:T(512)}, u32[]{:S(2)}) copy-start(f32[512]{0:T(512)} %copy-done.16) | copy-start | bytes 6148
  279.1 44.1 %copy-start.25 = (f32[1024]{0:T(1024)S(1)}, f32[1024]{0:T(1024)}, u32[]{:S(2)}) copy-start(f32[1024]{0:T(1024)} %param.21) | copy-start | bytes 12292
  279.1 2.1 copy-start.11
  282.5 2.7 copy-start.39
  285.2 3.0 copy-start.32
  293.5 2.7 copy-start.39
  296.2 3.0 copy-start.32
  304.5 2.7 copy-start.39
  307.2 3.0 copy-start.32
  315.5 2.7 copy-start.39
  318.2 3.0 copy-start.32
  323.2 7.5 %copy-start.19 = (f32[512]{0:T(512)S(1)}, f32[512]{0:T(512)}, u32[]{:S(2)}) copy-start(f32[512]{0:T(512)} %copy-done.18) | copy-start | bytes 6148
  323.2 7.5 %copy-start.31 = (bf16[4,512,4,64]{1,3,2,0:T(8,128)(2,1)S(1)}, bf16[4,512,4,64]{1,3,2,0:T(8,128)(2,1)}, u32[]{:S(2)}) copy-start(bf16[4,512,4,64]{1,3,2,0:T(8,128)(2,1)} %get-tuple-element.105) | copy-start | bytes 3145732
  323.2 7.5 %copy-start.34 = (bf16[4,512,4,64]{1,3,2,0:T(8,128)(2,1)S(1)}, bf16[4,512,4,64]{1,3,2,0:T(8,128)(2,1)}, u32[]{:S(2)}) copy-start(bf16[4,512,4,64]{1,3,2,0:T(8,128)(2,1)} %get-tuple-element.104) | copy-start | bytes 3145732
  323.2 7.5 %copy-start.37 = (f32[1024]{0:T(1024)S(1)}, f32[1024]{0:T(1024)}, u32[]{:S(2)}) copy-start(f32[1024]{0:T(1024)} %param.22) | copy-start | bytes 12292
  323.2 7.4 %copy-start.40 = (bf16[4,512,4,64]{1,3,2,0:T(8,128)(2,1)S(1)}, bf16[4,512,4,64]{1,3,2,0:T(8,128)(2,1)}, u32[]{:S(2)}) copy-start(bf16[4,512,4,64]{1,3,2,0:T(8,128)(2,1)} %get-tuple-element.106) | copy-start | bytes 3145732
  330.7 9.0 %copy-start.9 = (f32[512,1024]{1,0:T(8,128)}, f32[512,1024]{1,0:T(8,128)S(1)}, u32[]{:S(2)}) copy-start(f32[512,1024]{1,0:T(8,128)S(1)} %get-tuple-element.204) | copy-start | bytes 6291460
  330.7 8.9 %copy-start.23 = (f32[512]{0:T(512)S(1)}, f32[512]{0:T(512)}, u32[]{:S(2)}) copy-start(f32[512]{0:T(512)} %copy-done.22) | copy-start | bytes 6148
  355.8 222.9 %reduce-scatter.11.cloned.1.call-start = ((), (), s32[]{:S(2)}) async-start(), calls=%async_computation.11 | async-start | bytes 10485760 | tf_op jit(solution)/shard_map/reduce_scatter | solution.py:231
  373.8 294.4 %reduce-scatter.9.cloned.1.call-start = ((), (), s32[]{:S(2)}) async-start(), calls=%async_computation.10 | async-start | bytes 10485760 | tf_op jit(solution)/shard_map/reduce_scatter | solution.py:228
  406.2 81.2 %copy-start.28 = (s32[512]{0:T(512)S(1)}, s32[512]{0:T(512)}, u32[]{:S(2)}) copy-start(s32[512]{0:T(512)} %copy-done.27) | copy-start | bytes 6148
  406.2 79.8 %all-to-all-start.1 = ((bf16[8,128,1024]{2,1,0:T(8,128)(2,1)}), bf16[8,128,1024]{2,1,0:T(8,128)(2,1)S(1)}, u32[]{:S(2)}, u32[]{:S(2)}) async-start(bf16[8,128,1024]{2,1,0:T(8,128)(2,1)} %fusion.99), calls=%async_computation.1 | async-start | bytes 4194304 | tf_op jit(solution)/shard_map/all_to_all | solution.py:199
  410.0 289.2 %reduce-scatter.7.cloned.1.call-start = ((), (), s32[]{:S(2)}) async-start(), calls=%async_computation.9 | async-start | bytes 1351680 | tf_op jit(solution)/shard_map/reduce_scatter | solution.py:123
  487.4 4.7 copy-start.6
  487.4 4.7 copy-start.10
  487.4 4.7 copy-start.13
  487.4 4.7 copy-start.21
  578.8 125.3 %copy-start.1 = (bf16[1024,1024]{1,0:T(8,128)(2,1)S(1)}, bf16[1024,1024]{1,0:T(8,128)(2,1)}, u32[]{:S(2)}) copy-start(bf16[1024,1024]{1,0:T(8,128)(2,1)} %param.24) | copy-start | bytes 6291460
  (22 other events, 30.7 us)
Sparse Core Ops, SparseCore 0:
  355.9 120.8 reduce-scatter.4
  479.9 98.7 reduce-scatter.10
  581.8 86.3 reduce-scatter.8
  670.9 28.1 reduce-scatter.6

commit v2 on v0

v2 whole, which is shorter than its diff:
```python
import functools
import math

import jax
import jax.numpy as jnp
from jax import lax
from jax.experimental import pallas as pl
from jax.experimental.pallas import tpu as pltpu
from jax.sharding import PartitionSpec as P

HEADS = 16
GROUP = 4
LANES = 128
NEG_LARGE = -1e30
EPSILON = 1e-05
BF16 = jnp.bfloat16
F32 = jnp.float32


def dot_nn(a, b):
    return lax.dot_general(a, b, (((1,), (0,)), ((), ())), preferred_element_type=F32)


def dot_nt(a, b):
    return lax.dot_general(a, b, (((1,), (1,)), ((), ())), preferred_element_type=F32)


def dot_tn(a, b):
    return lax.dot_general(a, b, (((0,), (0,)), ((), ())), preferred_element_type=F32)


def iota(shape, axis):
    return lax.broadcasted_iota(jnp.int32, shape, axis)


def whole(shape):
    return pl.BlockSpec(shape, lambda *_: (0,) * len(shape))


def norm_parts(values):
    center = jnp.mean(values, -1, keepdims=True)
    centered = values - center
    spread = jnp.mean(centered * centered, -1, keepdims=True)
    factor = lax.rsqrt(spread + EPSILON)
    return centered * factor, factor


def norm_back(grad, gain, xhat, factor):
    scaled = grad * gain
    mean_scaled = jnp.mean(scaled, -1, keepdims=True)
    mean_cross = jnp.mean(scaled * xhat, -1, keepdims=True)
    return factor * (scaled - mean_scaled - xhat * mean_cross)


def slot_matrix(slot_row, slot_total):
    tok_rows = slot_row.shape[1]
    return (iota((slot_total, tok_rows), 0) == slot_row).astype(F32).astype(BF16)


def route_kernel(expert_count, capacity, ids_ref, table_ref, grad_ref, slot_ref, buffer_ref):
    tok_rows = ids_ref.shape[1]
    ids = ids_ref[...]
    table_rows = table_ref.shape[0]
    high = ids // LANES
    low = ids - high * LANES
    high_hot = (iota((table_rows, tok_rows), 0) == high).astype(F32).astype(BF16)
    picked = dot_tn(table_ref[...].astype(F32).astype(BF16), high_hot)
    low_hot = iota((LANES, tok_rows), 0) == low
    expert = jnp.sum(jnp.where(low_hot, picked, 0.0), 0, keepdims=True).astype(jnp.int32)
    expert_hot = (iota((expert_count, tok_rows), 0) == expert).astype(F32)
    before = (iota((tok_rows, tok_rows), 0) < iota((tok_rows, tok_rows), 1)).astype(F32)
    earlier = dot_nn(expert_hot.astype(BF16), before.astype(BF16))
    rank = jnp.sum(earlier * expert_hot, 0, keepdims=True).astype(jnp.int32)
    slot = expert * capacity + rank
    slot_ref[...] = slot
    slot_hot = slot_matrix(slot, expert_count * capacity)
    buffer_ref[...] = dot_nn(slot_hot, grad_ref[...]).astype(BF16)


def route(token_ids, hash_table, out_grad, expert_count, capacity):
    tok_rows, width = out_grad.shape
    slot_total = expert_count * capacity
    table_rows = hash_table.shape[0] // LANES
    return pl.pallas_call(
        functools.partial(route_kernel, expert_count, capacity),
        out_shape=(
            jax.ShapeDtypeStruct((1, tok_rows), jnp.int32),
            jax.ShapeDtypeStruct((slot_total, width), BF16),
        ),
        cost_estimate=pl.CostEstimate(
            flops=2 * slot_total * tok_rows * width, bytes_accessed=4 << 20, transcendentals=0
        ),
        name="route",
    )(token_ids.reshape(1, tok_rows), hash_table.reshape(table_rows, LANES), out_grad)


def front_kernel(
    slot_total,
    head_size,
    lengths_ref,
    tokens_ref,
    slot_ref,
    gain_one_ref,
    shift_one_ref,
    query_weight_ref,
    key_weight_ref,
    value_weight_ref,
    out_weight_ref,
    gain_two_ref,
    shift_two_ref,
    normed_ref,
    query_ref,
    key_ref,
    value_ref,
    probs_ref,
    mixture_ref,
    hidden_ref,
    buffer_ref,
    mask_ref,
):
    step = pl.program_id(0)
    tok_rows = tokens_ref.shape[0]
    group_width = query_ref.shape[1]

    @pl.when(step == 0)
    def _():
        inputs = tokens_ref[...].astype(F32)
        xhat, _ = norm_parts(inputs)
        normed_ref[...] = (xhat * gain_one_ref[...] + shift_one_ref[...]).astype(BF16)
        position = iota((1, tok_rows), 1)
        start = jnp.zeros((1, tok_rows), jnp.int32)
        bound = jnp.int32(0)
        for index in range(lengths_ref.shape[1]):
            bound = bound + lengths_ref[0, index]
            start = jnp.where(position >= bound, bound, start)
        key_position = iota((tok_rows, tok_rows), 0)
        allowed = jnp.logical_and(key_position >= start, key_position <= position)
        mask_ref[...] = jnp.where(allowed, 0.0, NEG_LARGE)
        hidden_ref[...] = inputs

    normed = normed_ref[...]
    query = dot_nn(normed, query_weight_ref[...]).astype(BF16)
    key = dot_nn(normed, key_weight_ref[...]).astype(BF16)
    value = dot_nn(normed, value_weight_ref[...]).astype(BF16)
    query_ref[...] = query
    key_ref[...] = key
    value_ref[...] = value
    lane_head = iota((1, group_width), 1) // head_size
    scale = 1.0 / math.sqrt(head_size)
    total = jnp.zeros((tok_rows, group_width), F32)
    for head in range(GROUP):
        chosen = lane_head == head
        key_part = key * jnp.where(chosen, scale, 0.0).astype(BF16)
        value_part = value * jnp.where(chosen, 1.0, 0.0).astype(BF16)
        scores = dot_nt(key_part, query) + mask_ref[...]
        exponent = jnp.exp(scores - jnp.max(scores, 0, keepdims=True))
        inverse = 1.0 / jnp.sum(exponent, 0, keepdims=True)
        weights = (exponent * inverse).astype(BF16)
        probs_ref[head] = weights
        total = total + dot_tn(weights, value_part)
    mixture = total.astype(BF16)
    mixture_ref[...] = mixture
    hidden_ref[...] += dot_nn(mixture, out_weight_ref[...])

    @pl.when(step == pl.num_programs(0) - 1)
    def _():
        xhat, _ = norm_parts(hidden_ref[...])
        routed = (xhat * gain_two_ref[...] + shift_two_ref[...]).astype(BF16)
        slot_hot = slot_matrix(slot_ref[...], slot_total)
        buffer_ref[...] = dot_nn(slot_hot, routed).astype(BF16)


def front(
    doc_lengths,
    tokens_in,
    slot_row,
    gain_one,
    shift_one,
    project_in,
    project_out,
    gain_two,
    shift_two,
    slot_total,
):
    tok_rows, width = tokens_in.shape
    head_size = width // HEADS
    group_width = GROUP * head_size
    steps = HEADS // GROUP
    vector = whole((1, width))

    def weight_spec(part):
        return pl.BlockSpec((width, group_width), lambda step: (0, part * steps + step))

    column_spec = pl.BlockSpec((tok_rows, group_width), lambda step: (0, step))
    return pl.pallas_call(
        functools.partial(front_kernel, slot_total, head_size),
        grid=(steps,),
        in_specs=[
            pl.BlockSpec(memory_space=pltpu.SMEM),
            whole((tok_rows, width)),
            whole((1, tok_rows)),
            vector,
            vector,
            weight_spec(0),
            weight_spec(1),
            weight_spec(2),
            pl.BlockSpec((group_width, width), lambda step: (step, 0)),
            vector,
            vector,
        ],
        out_specs=(
            whole((tok_rows, width)),
            column_spec,
            column_spec,
            column_spec,
            pl.BlockSpec((GROUP, tok_rows, tok_rows), lambda step: (step, 0, 0)),
            column_spec,
            whole((tok_rows, width)),
            whole((slot_total, width)),
        ),
        out_shape=(
            jax.ShapeDtypeStruct((tok_rows, width), BF16),
            jax.ShapeDtypeStruct((tok_rows, width), BF16),
            jax.ShapeDtypeStruct((tok_rows, width), BF16),
            jax.ShapeDtypeStruct((tok_rows, width), BF16),
            jax.ShapeDtypeStruct((HEADS, tok_rows, tok_rows), BF16),
            jax.ShapeDtypeStruct((tok_rows, width), BF16),
            jax.ShapeDtypeStruct((tok_rows, width), F32),
            jax.ShapeDtypeStruct((slot_total, width), BF16),
        ),
        scratch_shapes=[pltpu.VMEM((tok_rows, tok_rows), F32)],
        cost_estimate=pl.CostEstimate(
            flops=14 * 10**9, bytes_accessed=30 << 20, transcendentals=1 << 22
        ),
        name="front",
    )(
        doc_lengths,
        tokens_in,
        slot_row,
        gain_one.reshape(1, width),
        shift_one.reshape(1, width),
        project_in,
        project_in,
        project_in,
        project_out,
        gain_two.reshape(1, width),
        shift_two.reshape(1, width),
    )


def back_kernel(
    head_size,
    buffer_ref,
    slot_ref,
    hidden_ref,
    gain_two_ref,
    out_grad_ref,
    mixture_ref,
    out_weight_ref,
    query_ref,
    key_ref,
    value_ref,
    probs_ref,
    normed_ref,
    query_weight_ref,
    key_weight_ref,
    value_weight_ref,
    tokens_ref,
    gain_one_ref,
    dense_ref,
    small_ref,
    grad_in_ref,
    hidden_low_ref,
    normed_grad_ref,
):
    step = pl.program_id(0)
    width = tokens_ref.shape[1]
    group_width = query_ref.shape[1]

    @pl.when(step == 0)
    def _():
        slot_hot = slot_matrix(slot_ref[...], buffer_ref.shape[0])
        grad_routed = dot_tn(slot_hot, buffer_ref[...])
        xhat, factor = norm_parts(hidden_ref[...])
        small_ref[0:1, :] = jnp.sum(grad_routed * xhat, 0, keepdims=True)
        small_ref[1:2, :] = jnp.sum(grad_routed, 0, keepdims=True)
        grad_hidden = out_grad_ref[...].astype(F32) + norm_back(
            grad_routed, gain_two_ref[...], xhat, factor
        )
        grad_in_ref[...] = grad_hidden
        hidden_low_ref[...] = grad_hidden.astype(BF16)
        normed_grad_ref[...] = jnp.zeros_like(normed_grad_ref)

    hidden_low = hidden_low_ref[...]
    dense_ref[pl.ds(pl.multiple_of(step * group_width, group_width), group_width), 3 * width :] = (
        dot_tn(mixture_ref[...], hidden_low).astype(BF16)
    )
    grad_mixture = dot_nt(hidden_low, out_weight_ref[...]).astype(BF16)
    query, key, value = query_ref[...], key_ref[...], value_ref[...]
    lane_head = iota((1, group_width), 1) // head_size
    scale = 1.0 / math.sqrt(head_size)
    grad_query = jnp.zeros(query.shape, F32)
    grad_key = jnp.zeros(query.shape, F32)
    grad_value = jnp.zeros(query.shape, F32)
    for head in range(GROUP):
        chosen = jnp.where(lane_head == head, 1.0, 0.0).astype(BF16)
        scaled = jnp.where(lane_head == head, scale, 0.0).astype(BF16)
        grad_part = grad_mixture * chosen
        weights_low = probs_ref[head]
        weights = weights_low.astype(F32)
        grad_weights = dot_nt(value, grad_part)
        inner = jnp.sum(weights * grad_weights, 0, keepdims=True)
        grad_scores = (weights * (grad_weights - inner)).astype(BF16)
        grad_query = grad_query + dot_tn(grad_scores, key * scaled)
        grad_key = grad_key + dot_nn(grad_scores, query * scaled)
        grad_value = grad_value + dot_nn(weights_low, grad_part)
    normed = normed_ref[...]
    for part, (grad, weight_ref) in enumerate(
        (
            (grad_query, query_weight_ref),
            (grad_key, key_weight_ref),
            (grad_value, value_weight_ref),
        )
    ):
        grad = grad.astype(BF16)
        column = pl.multiple_of(part * width + step * group_width, group_width)
        dense_ref[:, pl.ds(column, group_width)] = dot_tn(normed, grad).astype(BF16)
        normed_grad_ref[...] += dot_nt(grad, weight_ref[...])

    @pl.when(step == pl.num_programs(0) - 1)
    def _():
        grad_normed = normed_grad_ref[...]
        xhat, factor = norm_parts(tokens_ref[...].astype(F32))
        small_ref[2:3, :] = jnp.sum(grad_normed * xhat, 0, keepdims=True)
        small_ref[3:4, :] = jnp.sum(grad_normed, 0, keepdims=True)
        small_ref[4:8, :] = jnp.zeros((4, width), F32)
        grad_in_ref[...] += norm_back(grad_normed, gain_one_ref[...], xhat, factor)


def back(
    grad_buffer,
    slot_row,
    hidden,
    gain_two,
    out_grad,
    mixture,
    project_out,
    query,
    key,
    value,
    probs,
    normed,
    project_in,
    tokens_in,
    gain_one,
):
    tok_rows, width = tokens_in.shape
    head_size = width // HEADS
    group_width = GROUP * head_size
    steps = HEADS // GROUP
    vector = whole((1, width))
    tokens_spec = whole((tok_rows, width))

    def weight_spec(part):
        return pl.BlockSpec((width, group_width), lambda step: (0, part * steps + step))

    column_spec = pl.BlockSpec((tok_rows, group_width), lambda step: (0, step))
    return pl.pallas_call(
        functools.partial(back_kernel, head_size),
        grid=(steps,),
        in_specs=[
            whole(grad_buffer.shape),
            whole((1, tok_rows)),
            tokens_spec,
            vector,
            tokens_spec,
            column_spec,
            pl.BlockSpec((group_width, width), lambda step: (step, 0)),
            column_spec,
            column_spec,
            column_spec,
            pl.BlockSpec((GROUP, tok_rows, tok_rows), lambda step: (step, 0, 0)),
            tokens_spec,
            weight_spec(0),
            weight_spec(1),
            weight_spec(2),
            tokens_spec,
            vector,
        ],
        out_specs=(
            whole((width, 4 * width)),
            whole((8, width)),
            tokens_spec,
        ),
        out_shape=(
            jax.ShapeDtypeStruct((width, 4 * width), BF16),
            jax.ShapeDtypeStruct((8, width), F32),
            jax.ShapeDtypeStruct((tok_rows, width), F32),
        ),
        scratch_shapes=[
            pltpu.VMEM((tok_rows, width), BF16),
            pltpu.VMEM((tok_rows, width), F32),
        ],
        cost_estimate=pl.CostEstimate(
            flops=24 * 10**9, bytes_accessed=50 << 20, transcendentals=0
        ),
        name="back",
    )(
        grad_buffer,
        slot_row,
        hidden,
        gain_two.reshape(1, width),
        out_grad,
        mixture,
        project_out,
        query,
        key,
        value,
        probs,
        normed,
        project_in,
        project_in,
        project_in,
        tokens_in,
        gain_one.reshape(1, width),
    )


def finish_kernel(hidden_ref, slot_ref, buffer_ref, out_ref):
    slot_hot = slot_matrix(slot_ref[...], buffer_ref.shape[0])
    out_ref[...] = (hidden_ref[...] + dot_tn(slot_hot, buffer_ref[...])).astype(BF16)


def finish(hidden, slot_row, buffer):
    return pl.pallas_call(
        finish_kernel,
        out_shape=jax.ShapeDtypeStruct(hidden.shape, BF16),
        cost_estimate=pl.CostEstimate(
            flops=10**9, bytes_accessed=5 << 20, transcendentals=0
        ),
        name="finish",
    )(hidden, slot_row, buffer)


def exchange(buffer, expert_count):
    shape = buffer.shape
    buffer = buffer.reshape(expert_count, shape[0] // expert_count, shape[1])
    buffer = lax.all_to_all(buffer, "ep", split_axis=0, concat_axis=0, tiled=True)
    return buffer.reshape(shape)


def smooth_gate(values):
    return jax.nn.gelu(values, approximate=True)


def local(
    tokens_in,
    token_ids,
    hash_table,
    doc_lengths,
    gain_one,
    shift_one,
    project_in,
    project_out,
    gain_two,
    shift_two,
    expert_in,
    expert_out,
    out_grad,
):
    tok_rows, width = tokens_in.shape
    expert_count = expert_in.shape[0] * lax.axis_size("ep")
    capacity = 2 * tok_rows // expert_count
    slot_total = expert_count * capacity
    first_weight, second_weight = expert_in[0], expert_out[0]

    slot_row, grad_buffer = route(token_ids, hash_table, out_grad, expert_count, capacity)
    grad_received = exchange(grad_buffer, expert_count)
    normed, query, key, value, probs, mixture, hidden, buffer = front(
        doc_lengths,
        tokens_in,
        slot_row,
        gain_one,
        shift_one,
        project_in,
        project_out,
        gain_two,
        shift_two,
        slot_total,
    )
    received = exchange(buffer, expert_count)
    grad_act = jnp.einsum("sd,fd->sf", grad_received, second_weight, preferred_element_type=F32)
    grad_act = grad_act.astype(BF16)
    pre_act = jnp.einsum("sd,df->sf", received, first_weight, preferred_element_type=F32)
    gate_value, gate_pull = jax.vjp(smooth_gate, pre_act)
    activation = gate_value.astype(BF16)
    grad_pre = gate_pull(grad_act.astype(F32))[0].astype(BF16)
    grad_routed = jnp.einsum(
        "sf,df->sd", grad_pre, first_weight, preferred_element_type=F32
    ).astype(BF16)
    grad_back = exchange(grad_routed, expert_count)
    grad_second = jnp.einsum(
        "sf,sd->fd", activation, grad_received, preferred_element_type=F32
    ).astype(BF16)
    grad_first = jnp.einsum("sd,sf->df", received, grad_pre, preferred_element_type=F32).astype(
        BF16
    )
    summed_second = lax.psum_scatter(grad_second, "rep", scatter_dimension=0, tiled=True)
    summed_first = lax.psum_scatter(grad_first, "rep", scatter_dimension=0, tiled=True)
    result = jnp.einsum(
        "sf,fd->sd", activation, second_weight, preferred_element_type=F32
    ).astype(BF16)
    grad_back, grad_second, grad_first, result = lax.optimization_barrier(
        (grad_back, grad_second, grad_first, result)
    )
    returned = exchange(result, expert_count)
    dense, small, grad_in = back(
        grad_back,
        slot_row,
        hidden,
        gain_two,
        out_grad,
        mixture,
        project_out,
        query,
        key,
        value,
        probs,
        normed,
        project_in,
        tokens_in,
        gain_one,
    )
    columns = jnp.pad(small, ((0, LANES - small.shape[0]), (0, 0))).T.astype(BF16)
    dense = jnp.concatenate([dense, columns], 1)
    dense = lax.psum_scatter(dense, "rep", scatter_dimension=0, tiled=True)
    dense = lax.psum_scatter(dense, "ep", scatter_dimension=0, tiled=True).astype(F32)
    block_out = finish(hidden, slot_row, returned)
    return (
        block_out,
        grad_in,
        dense[:, : 3 * width],
        dense[:, 3 * width : 4 * width],
        dense[:, 4 * width + 2],
        dense[:, 4 * width + 3],
        dense[:, 4 * width],
        dense[:, 4 * width + 1],
        summed_first.astype(F32)[None],
        summed_second.astype(F32)[None],
    )


def solution(mesh):
    in_specs = (
        P(("rep", "ep"), None),
        P(("rep", "ep")),
        P(),
        P(("rep", "ep"), None),
        P(),
        P(),
        P(),
        P(),
        P(),
        P(),
        P("ep", None, None),
        P("ep", None, None),
        P(("rep", "ep"), None),
    )
    out_specs = (
        P(("rep", "ep"), None),
        P(("rep", "ep"), None),
        P(("rep", "ep"), None),
        P(("rep", "ep"), None),
        P(("rep", "ep")),
        P(("rep", "ep")),
        P(("rep", "ep")),
        P(("rep", "ep")),
        P("ep", "rep", None),
        P("ep", "rep", None),
    )
    return jax.shard_map(local, mesh=mesh, in_specs=in_specs, out_specs=out_specs, check_vma=False)
```

time: 804 us -> 623 us (0.77); the launches traced: 789 us -> 617 us
  local copies, waits for them, and re-layouts: 199 us -> 6.79 us
  matrix products: 196 us -> 104 us
  Pallas kernels: 0 us -> 68.7 us
  waiting for transfers between devices: 282 us -> 339 us
  other arithmetic: 39 us -> 17.4 us
  blocking collectives: 37.7 us -> 55.4 us
    scatter x2 -> x0, local copies, waits for them, and re-layouts: 149 us -> none  [the longest x1 74.3 us: local(): dispatch_buffer = jnp.zeros((expert_count, capacity, model_width), jnp.bf...]
    reduce_scatter x4, waiting for transfers between devices: 177 us -> 285 us  [the longest x1 85.3 us: local(): lax.psum_scatter(grad_first, 'rep', scatter_dimension=0, tiled=True)]
    dot_general x40 -> x6, matrix products: 196 us -> 104 us  [the longest x1 24.8 us: local(): jnp.einsum('sd,fd->sf', grad_received, second_weight, preferred_element_t...]
    pallas_call x0 -> x4, Pallas kernels: none -> 68.7 us  [the longest x1 37.5 us: back(): pl.pallas_call(functools.partial(back_kernel, head_size), grid=(steps,),...]
    all_to_all x0 -> x1, blocking collectives: none -> 55.4 us  [exchange(): lax.all_to_all(buffer, 'ep', split_axis=0, concat_axis=0, tiled=True)]
    all_to_all x4 -> x3, waiting for transfers between devices: 105 us -> 51.6 us  [exchange(): lax.all_to_all(buffer, 'ep', split_axis=0, concat_axis=0, tiled=True)]
    unnamed x1 -> x0, blocking collectives: 37.7 us -> none
    gather x3 -> x0, local copies, waits for them, and re-layouts: 21.9 us -> none  [the longest x1 10.7 us: local(): block_sum = hidden + returned[expert_ids, slot_rank].astype(jnp.float32)]
  transfers between devices with their start and end apart: 8 -> 7, of which waited for: 5 -> 6; matrix products, arithmetic and copies ran while one was open for 35% -> 9% of each run, Pallas kernels for 0% -> 1%
where the time goes in v2:
time: 623 us; the launch traced here: 617 us
  waiting for transfers between devices  339 us (54%)
  matrix products  104 us (17%)
  Pallas kernels  68.7 us (11%)
  blocking collectives  55.4 us (9%)
  other arithmetic  17.4 us (3%)
  between operations  14.3 us (2%)
  starting transfers between devices  12.4 us (2%)
  local copies, waits for them, and re-layouts  6.79 us (1%)
    reduce_scatter x1, waiting for transfers between devices, local(): lax.psum_scatter(grad_first, 'rep', scatter_dimension=0, tiled=True)  85.3 us
    reduce_scatter x1, waiting for transfers between devices, local(): lax.psum_scatter(grad_second, 'rep', scatter_dimension=0, tiled=True)  83.6 us
    reduce_scatter x1, waiting for transfers between devices, local(): dense = lax.psum_scatter(dense, 'rep', scatter_dimension=0, tiled=True)  82.3 us
    all_to_all x1, blocking collectives, exchange(): lax.all_to_all(buffer, 'ep', split_axis=0, concat_axis=0, tiled=True)  55.4 us
    all_to_all x3, waiting for transfers between devices, exchange(): lax.all_to_all(buffer, 'ep', split_axis=0, concat_axis=0, tiled=True)  51.6 us
    pallas_call x1, Pallas kernels, back(): pl.pallas_call(functools.partial(back_kernel, head_size), grid=(steps,),...  37.5 us
    reduce_scatter x1, waiting for transfers between devices, local(): lax.psum_scatter(dense, 'ep', scatter_dimension=0, tiled=True).astype(F32)  34.3 us
    dot_general x1, matrix products, local(): jnp.einsum('sd,fd->sf', grad_received, second_weight, preferred_element_t...  24.8 us
  transfers between devices with their start and end apart: 7, of which 6 were waited for; matrix products, arithmetic and copies ran while one was open for 9% of the time, Pallas kernels for 1%

profile of v2, /device:TPU:0, one launch (start us, length us, event | category | flops | bytes accessed | tf_op | source)
XLA Modules:
  0.0 617.2 jit_solution(14161979984554604061)
XLA Ops:
  7.2 4.2 route.1
  11.3 22.5 %front.1 = (bf16[512,1024]{1,0:T(8,128)(2,1)}, bf16[512,1024]{1,0:T(8,128)(2,1)}, bf16[512,1024]{1,0:T(8,128)(2,1)}, bf16[512,1024]{1,0:T(8,128)(2,1)}, bf16[16,...) custom-call(s32[1,4]{1,0:T(1,128)} %lengths_ref.1, ...), custom_call_target="tpu_custom_call" | custom-call | flops 14000000000 | bytes 31457280 | tf_op jit(solution)/shard_map/front/pallas_call | solution.py:195
  33.9 55.4 %all_to_all.20 = bf16[8,128,1024]{2,1,0:T(8,128)(2,1)S(1)} all-to-all(bf16[8,128,1024]{2,1,0:T(8,128)(2,1)} %bitcast.51), channel_id=1, replica_groups=mesh['rep'=4,'ep'=8] {'ep'}, dimensions={0} | all-to-all | bytes 4194304 | tf_op jit(solution)/shard_map/all_to_all | solution.py:448
  89.3 0.0 copy-start.2
  89.3 4.8 all-to-all-start
  94.1 14.4 %fusion.12 = f32[1024,4096]{1,0:T(8,128)} fusion(bf16[1024,1024]{1,0:T(8,128)(2,1)S(1)} %bitcast.47, bf16[1,1024,4096]{2,1,0:T(8,128)(2,1)} %param.23), kind=kOutput, calls=%fused_computation.18 | convolution fusion | flops 8589934592 | bytes 27262976 | tf_op jit(solution)/shard_map/sd,df->sf/dot_general | solution.py:494
  108.5 0.0 copy-done.2
  108.5 34.6 %all-to-all-done = bf16[8,128,1024]{2,1,0:T(8,128)(2,1)} async-done(((bf16[8,128,1024]{2,1,0:T(8,128)(2,1)}), bf16[8,128,1024]{2,1,0:T(8,128)(2,1)}, u32[]{:S(2)}, u32[]{:S(2)}) %all-to-all-start) | async-done | bytes 2097184 | tf_op jit(solution)/shard_map/all_to_all | solution.py:448
  143.1 17.9 %convolution_convert_fusion.1 = bf16[4096,1024]{1,0:T(8,128)(2,1)} fusion(bf16[1024,1024]{1,0:T(8,128)(2,1)} %bitcast.7, f32[1024,4096]{1,0:T(8,128)} %fusion.12), kind=kOutput, calls=%fused_computation.25 | convolution fusion | flops 8631877632 | bytes 27262976 | tf_op jit(solution)/shard_map/sf,sd->fd/dot_general | solution.py:502
  161.0 24.8 %fusion.2 = bf16[1024,4096]{1,0:T(8,128)(2,1)} fusion(f32[1024,4096]{1,0:T(8,128)} %fusion.12, bf16[1024,1024]{1,0:T(8,128)(2,1)} %bitcast.7, bf16[1,4096,1024]{2,1,0:T(8,128)(2,1)} %param.24), kind=kOutput, calls=%fused_computation.6 | convolution fusion | flops 8682209280 | bytes 35651584 | tf_op jit(solution)/shard_map/sd,fd->sf/dot_general | solution.py:492
  185.8 14.7 %fusion.23 = bf16[1024,1024]{1,0:T(8,128)(2,1)} fusion(bf16[1024,4096]{1,0:T(8,128)(2,1)} %fusion.2, bf16[1,1024,4096]{2,1,0:T(8,128)(2,1)} %param.23), kind=kOutput, calls=%fused_computation.29 | convolution fusion | flops 8590983168 | bytes 18874368 | tf_op jit(solution)/shard_map/sf,df->sd/dot_general | solution.py:498
  200.5 3.8 all-to-all-start.2
  204.4 0.0 reduce-scatter.5.cloned.1.call-start
  204.4 14.8 %convolution_convert_fusion = bf16[1024,4096]{1,0:T(8,128)(2,1)} fusion(bf16[1024,1024]{1,0:T(8,128)(2,1)} %bitcast.48, bf16[1024,4096]{1,0:T(8,128)(2,1)} %fusion.2), kind=kOutput, calls=%fused_computation.24 | convolution fusion | flops 8594128896 | bytes 18874368 | tf_op jit(solution)/shard_map/sd,sf->df/dot_general | solution.py:505
  219.2 17.0 %fusion.20 = bf16[1024,1024]{1,0:T(8,128)(2,1)} fusion(bf16[1,4096,1024]{2,1,0:T(8,128)(2,1)} %param.24, f32[1024,4096]{1,0:T(8,128)} %fusion.12), kind=kOutput, calls=%fused_computation.28 | convolution fusion | flops 8628731904 | bytes 27262976 | tf_op jit(solution)/shard_map/sf,fd->sd/dot_general | solution.py:510
  236.3 17.0 %all-to-all-done.2 = bf16[8,128,1024]{2,1,0:T(8,128)(2,1)S(1)} async-done(((bf16[8,128,1024]{2,1,0:T(8,128)(2,1)}), bf16[8,128,1024]{2,1,0:T(8,128)(2,1)S(1)}, u32[]{:S(2)}, u32[]{:S(2)}) %all-to-all-start.2) | async-done | bytes 2097184 | tf_op jit(solution)/shard_map/all_to_all | solution.py:448
  253.3 0.0 copy-start.1
  253.3 1.3 copy-done.1
  254.6 37.5 %back.1 = (bf16[1024,4096]{1,0:T(8,128)(2,1)}, f32[8,1024]{1,0:T(8,128)}, f32[512,1024]{1,0:T(8,128)}) custom-call(bf16[1024,1024]{1,0:T(8,128)(2,1)} %bitcast.46, s32[1,512]{1,0:T(1,128)} %get-tuple-element.25.slot_ref, f32[512,1024]{1,0:T(8,128)} %get-tuple-element.26.hidden_ref, f32[1,1024]{1,0:T(1,128)} %bitcast.58, bf16[512,1024]{1,0:T(8,128)(2,1)} %out_grad_ref.1, ...), custom_call_target="tpu_custom_call" | custom-call | flops 24000000000 | bytes 52428800 | tf_op jit(solution)/shard_map/back/pallas_call | solution.py:368
  292.2 0.8 convert.6
  293.0 0.2 copy.24
  293.1 7.4 %pad_maximum_fusion = bf16[1024,4224]{1,0:T(8,128)(2,1)} fusion(bf16[1024,128]{1,0:T(8,128)(2,1)S(1)} %copy.24, bf16[1024,4096]{1,0:T(8,128)(2,1)} %get-tuple-element.38), kind=kLoop, calls=%fused_computation.15 | loop fusion | flops 17301504 | bytes 17301504 | tf_op jit(solution)/shard_map/concatenate | solution.py:535
  300.6 0.0 reduce-scatter.5.cloned.1.call-update
  300.6 0.0 reduce-scatter.11.cloned.1.call-start
  300.7 0.7 reduce-scatter.11.cloned.1.call-update
  301.4 0.0 reduce-scatter.9.cloned.1.call-start
  301.4 0.7 reduce-scatter.9.cloned.1.call-update
  302.1 3.6 all-to-all-start.3
  305.7 0.0 reduce-scatter.7.cloned.1.call-start
  305.8 82.3 %reduce-scatter.5.cloned.1.call-done = bf16[256,4224]{1,0:T(8,128)(2,1)} async-done(((bf16[1024,4224]{1,0:T(8,128)(2,1)}), bf16[256,4224]{1,0:T(8,128)(2,1)}) %reduce-scatter.5.cloned.1.call-update) | async-done | bytes 2162704 | tf_op jit(solution)/shard_map/reduce_scatter | solution.py:536
  388.1 0.0 reduce-scatter.7.cloned.1.call-update
  388.1 0.0 all-to-all-done.3
  388.1 0.0 copy-start
  388.2 1.3 copy-done
  389.5 4.5 finish.1
  394.0 83.6 %reduce-scatter.11.cloned.1.call-done = bf16[1024,1024]{1,0:T(8,128)(2,1)} async-done(((bf16[4096,1024]{1,0:T(8,128)(2,1)}), bf16[1024,1024]{1,0:T(8,128)(2,1)}) %reduce-scatter.11.cloned.1.call-update) | async-done | bytes 2097168 | tf_op jit(solution)/shard_map/reduce_scatter | solution.py:508
  477.5 4.1 bitcast_convert_fusion
  481.6 85.3 %reduce-scatter.9.cloned.1.call-done = bf16[256,4096]{1,0:T(8,128)(2,1)} async-done(((bf16[1024,4096]{1,0:T(8,128)(2,1)}), bf16[256,4096]{1,0:T(8,128)(2,1)}) %reduce-scatter.9.cloned.1.call-update) | async-done | bytes 2097168 | tf_op jit(solution)/shard_map/reduce_scatter | solution.py:509
  566.9 4.1 bitcast_convert_fusion.1
  571.0 34.3 %reduce-scatter.7.cloned.1.call-done = bf16[32,4224]{1,0:T(8,128)(2,1)} async-done(((bf16[256,4224]{1,0:T(8,128)(2,1)}), bf16[32,4224]{1,0:T(8,128)(2,1)}) %reduce-scatter.7.cloned.1.call-update) | async-done | bytes 270352 | tf_op jit(solution)/shard_map/reduce_scatter | solution.py:537
  605.3 1.0 convert_element_type.44
  606.3 0.7 slice_reduce_fusion
  607.0 1.7 slice.24
  608.7 1.5 slice.25
  (1 shorter events, 0.0 us)
Async XLA Ops:
  89.3 19.3 %copy-start.2 = (bf16[8,128,1024]{2,1,0:T(8,128)(2,1)}, bf16[8,128,1024]{2,1,0:T(8,128)(2,1)S(1)}, u32[]{:S(2)}) copy-start(bf16[8,128,1024]{2,1,0:T(8,128)(2,1)S(1)} %all_to_all.20) | copy-start | bytes 6291460
  89.3 53.9 %all-to-all-start = ((bf16[8,128,1024]{2,1,0:T(8,128)(2,1)}), bf16[8,128,1024]{2,1,0:T(8,128)(2,1)}, u32[]{:S(2)}, u32[]{:S(2)}) async-start(bf16[8,128,1024]{2,1,0:T(8,128)(2,1)} %bitcast.49), calls=%async_computation | async-start | bytes 4194304 | tf_op jit(solution)/shard_map/all_to_all | solution.py:448
  200.5 52.8 %all-to-all-start.2 = ((bf16[8,128,1024]{2,1,0:T(8,128)(2,1)}), bf16[8,128,1024]{2,1,0:T(8,128)(2,1)S(1)}, u32[]{:S(2)}, u32[]{:S(2)}) async-start(bf16[8,128,1024]{2,1,0:T(8,128)(2,1)} %bitcast.50), calls=%async_computation.2 | async-start | bytes 4194304 | tf_op jit(solution)/shard_map/all_to_all | solution.py:448
  204.4 183.8 %reduce-scatter.5.cloned.1.call-start = ((), (), s32[]{:S(2)}) async-start(), calls=%async_computation.8 | async-start | bytes 10813440 | tf_op jit(solution)/shard_map/reduce_scatter | solution.py:536
  253.3 1.3 copy-start.1
  300.6 176.9 %reduce-scatter.11.cloned.1.call-start = ((), (), s32[]{:S(2)}) async-start(), calls=%async_computation.11 | async-start | bytes 10485760 | tf_op jit(solution)/shard_map/reduce_scatter | solution.py:508
  301.4 265.6 %reduce-scatter.9.cloned.1.call-start = ((), (), s32[]{:S(2)}) async-start(), calls=%async_computation.10 | async-start | bytes 10485760 | tf_op jit(solution)/shard_map/reduce_scatter | solution.py:509
  302.1 86.0 %all-to-all-start.3 = ((bf16[8,128,1024]{2,1,0:T(8,128)(2,1)}), bf16[8,128,1024]{2,1,0:T(8,128)(2,1)S(1)}, u32[]{:S(2)}, u32[]{:S(2)}) async-start(bf16[8,128,1024]{2,1,0:T(8,128)(2,1)} %bitcast.45), calls=%async_computation.3 | async-start | bytes 4194304 | tf_op jit(solution)/shard_map/all_to_all | solution.py:448
  305.7 299.6 %reduce-scatter.7.cloned.1.call-start = ((), (), s32[]{:S(2)}) async-start(), calls=%async_computation.9 | async-start | bytes 2433024 | tf_op jit(solution)/shard_map/reduce_scatter | solution.py:537
  388.1 1.3 copy-start
Sparse Core Ops, SparseCore 0:
  300.7 87.3 reduce-scatter.4
  391.2 86.3 reduce-scatter.10
  480.6 86.2 reduce-scatter.8
  569.1 36.1 reduce-scatter.6

commit v3 on v2

--- a/solution.py
+++ b/solution.py
@@ -15,6 +15,8 @@
 EPSILON = 1e-05
 BF16 = jnp.bfloat16
 F32 = jnp.float32
+GATE_A = math.sqrt(2.0 / math.pi)
+GATE_B = GATE_A * 0.044715
 
 
 def dot_nn(a, b):
@@ -57,7 +59,9 @@
     return (iota((slot_total, tok_rows), 0) == slot_row).astype(F32).astype(BF16)
 
 
-def route_kernel(expert_count, capacity, ids_ref, table_ref, grad_ref, slot_ref, buffer_ref):
+def route_kernel(
+    expert_count, capacity, flip_ref, ids_ref, table_ref, grad_ref, slot_ref, buffer_ref
+):
     tok_rows = ids_ref.shape[1]
     ids = ids_ref[...]
     table_rows = table_ref.shape[0]
@@ -71,18 +75,25 @@
     before = (iota((tok_rows, tok_rows), 0) < iota((tok_rows, tok_rows), 1)).astype(F32)
     earlier = dot_nn(expert_hot.astype(BF16), before.astype(BF16))
     rank = jnp.sum(earlier * expert_hot, 0, keepdims=True).astype(jnp.int32)
-    slot = expert * capacity + rank
+    slot = (expert ^ flip_ref[0]) * capacity + rank
     slot_ref[...] = slot
     slot_hot = slot_matrix(slot, expert_count * capacity)
     buffer_ref[...] = dot_nn(slot_hot, grad_ref[...]).astype(BF16)
 
 
-def route(token_ids, hash_table, out_grad, expert_count, capacity):
+def route(flip, token_ids, hash_table, out_grad, expert_count, capacity):
     tok_rows, width = out_grad.shape
     slot_total = expert_count * capacity
     table_rows = hash_table.shape[0] // LANES
     return pl.pallas_call(
         functools.partial(route_kernel, expert_count, capacity),
+        in_specs=[
+            pl.BlockSpec(memory_space=pltpu.SMEM),
+            whole((1, tok_rows)),
+            whole((table_rows, LANES)),
+            whole((tok_rows, width)),
+        ],
+        out_specs=(whole((1, tok_rows)), whole((slot_total, width))),
         out_shape=(
             jax.ShapeDtypeStruct((1, tok_rows), jnp.int32),
             jax.ShapeDtypeStruct((slot_total, width), BF16),
@@ -91,7 +102,7 @@
             flops=2 * slot_total * tok_rows * width, bytes_accessed=4 << 20, transcendentals=0
         ),
         name="route",
-    )(token_ids.reshape(1, tok_rows), hash_table.reshape(table_rows, LANES), out_grad)
+    )(flip, token_ids.reshape(1, tok_rows), hash_table.reshape(table_rows, LANES), out_grad)
 
 
 def front_kernel(
@@ -248,8 +259,25 @@
     )
 
 
+def spread_bits(index, layout):
+    spot = 0
+    for place, bit in enumerate(layout):
+        spot = spot | (((index >> bit) & 1) << place)
+    return spot
+
+
+def store_rows(dense_ref, first, column, values, tile, layout, spot):
+    for index in range(values.shape[0] // tile):
+        place = spread_bits(first + index, layout) ^ spot
+        row = pl.multiple_of(place * tile, tile)
+        dense_ref[pl.ds(row, tile), column] = values[index * tile : (index + 1) * tile]
+
+
 def back_kernel(
     head_size,
+    tile,
+    layout,
+    spot_ref,
     buffer_ref,
     slot_ref,
     hidden_ref,
@@ -268,10 +296,10 @@
     tokens_ref,
     gain_one_ref,
     dense_ref,
-    small_ref,
     grad_in_ref,
     hidden_low_ref,
     normed_grad_ref,
+    small_ref,
 ):
     step = pl.program_id(0)
     width = tokens_ref.shape[1]
@@ -290,10 +318,18 @@
         grad_in_ref[...] = grad_hidden
         hidden_low_ref[...] = grad_hidden.astype(BF16)
         normed_grad_ref[...] = jnp.zeros_like(normed_grad_ref)
+        small_ref[4:, :] = jnp.zeros((LANES - 4, width), F32)
 
     hidden_low = hidden_low_ref[...]
-    dense_ref[pl.ds(pl.multiple_of(step * group_width, group_width), group_width), 3 * width :] = (
-        dot_tn(mixture_ref[...], hidden_low).astype(BF16)
+    spot = spot_ref[0]
+    store_rows(
+        dense_ref,
+        step * (group_width // tile),
+        slice(3 * width, 4 * width),
+        dot_tn(mixture_ref[...], hidden_low).astype(BF16),
+        tile,
+        layout,
+        spot,
     )
     grad_mixture = dot_nt(hidden_low, out_weight_ref[...]).astype(BF16)
     query, key, value = query_ref[...], key_ref[...], value_ref[...]
@@ -324,7 +360,15 @@
     ):
         grad = grad.astype(BF16)
         column = pl.multiple_of(part * width + step * group_width, group_width)
-        dense_ref[:, pl.ds(column, group_width)] = dot_tn(normed, grad).astype(BF16)
+        store_rows(
+            dense_ref,
+            0,
+            pl.ds(column, group_width),
+            dot_tn(normed, grad).astype(BF16),
+            tile,
+            layout,
+            spot,
+        )
         normed_grad_ref[...] += dot_nt(grad, weight_ref[...])
 
     @pl.when(step == pl.num_programs(0) - 1)
@@ -333,11 +377,22 @@
         xhat, factor = norm_parts(tokens_ref[...].astype(F32))
         small_ref[2:3, :] = jnp.sum(grad_normed * xhat, 0, keepdims=True)
         small_ref[3:4, :] = jnp.sum(grad_normed, 0, keepdims=True)
-        small_ref[4:8, :] = jnp.zeros((4, width), F32)
+        store_rows(
+            dense_ref,
+            0,
+            slice(4 * width, 4 * width + LANES),
+            small_ref[...].T.astype(BF16),
+            tile,
+            layout,
+            spot,
+        )
         grad_in_ref[...] += norm_back(grad_normed, gain_one_ref[...], xhat, factor)
 
 
 def back(
+    tile,
+    layout,
+    spot,
     grad_buffer,
     slot_row,
     hidden,
@@ -366,9 +421,10 @@
 
     column_spec = pl.BlockSpec((tok_rows, group_width), lambda step: (0, step))
     return pl.pallas_call(
-        functools.partial(back_kernel, head_size),
+        functools.partial(back_kernel, head_size, tile, layout),
         grid=(steps,),
         in_specs=[
+            pl.BlockSpec(memory_space=pltpu.SMEM),
             whole(grad_buffer.shape),
             whole((1, tok_rows)),
             tokens_spec,
@@ -388,24 +444,24 @@
             vector,
         ],
         out_specs=(
-            whole((width, 4 * width)),
-            whole((8, width)),
+            whole((width, 4 * width + LANES)),
             tokens_spec,
         ),
         out_shape=(
-            jax.ShapeDtypeStruct((width, 4 * width), BF16),
-            jax.ShapeDtypeStruct((8, width), F32),
+            jax.ShapeDtypeStruct((width, 4 * width + LANES), BF16),
             jax.ShapeDtypeStruct((tok_rows, width), F32),
         ),
         scratch_shapes=[
             pltpu.VMEM((tok_rows, width), BF16),
             pltpu.VMEM((tok_rows, width), F32),
+            pltpu.VMEM((LANES, width), F32),
         ],
         cost_estimate=pl.CostEstimate(
             flops=24 * 10**9, bytes_accessed=50 << 20, transcendentals=0
         ),
         name="back",
     )(
+        spot,
         grad_buffer,
         slot_row,
         hidden,
@@ -442,15 +498,206 @@
     )(hidden, slot_row, buffer)
 
 
+def gate_parts(pre):
+    square = pre * pre
+    curve = jnp.tanh(pre * (GATE_A + GATE_B * square))
+    half = 0.5 * curve + 0.5
+    slope = half + (0.5 * pre) * (1.0 - curve * curve) * (GATE_A + (3.0 * GATE_B) * square)
+    return pre * half, slope
+
+
+def expert_kernel(
+    tile, routed_ref, grad_act_ref, weight_ref, act_ref, grad_pre_ref, out_ref, total_ref
+):
+    step = pl.program_id(0)
+
+    @pl.when(step == 0)
+    def _():
+        total_ref[...] = jnp.zeros_like(total_ref)
+
+    weight = weight_ref[...]
+    for first in range(0, routed_ref.shape[0], tile):
+        rows = slice(first, first + tile)
+        act, slope = gate_parts(dot_nn(routed_ref[rows, :], weight))
+        act_ref[rows, :] = act.astype(BF16)
+        grad_pre = (grad_act_ref[rows, :].astype(F32) * slope).astype(BF16)
+        grad_pre_ref[rows, :] = grad_pre
+        total_ref[rows, :] += dot_nt(grad_pre, weight)
+
+    @pl.when(step == pl.num_programs(0) - 1)
+    def _():
+        out_ref[...] = total_ref[...].astype(BF16)
+
+
+def expert(routed, grad_act, weight, chunk=1024, tile=256):
+    rows, width = routed.shape
+    hidden_units = weight.shape[1]
+    column_spec = pl.BlockSpec((rows, chunk), lambda step: (0, step))
+    return pl.pallas_call(
+        functools.partial(expert_kernel, tile),
+        grid=(hidden_units // chunk,),
+        in_specs=[
+            whole((rows, width)),
+            column_spec,
+            pl.BlockSpec((width, chunk), lambda step: (0, step)),
+        ],
+        out_specs=(column_spec, column_spec, whole((rows, width))),
+        out_shape=(
+            jax.ShapeDtypeStruct((rows, hidden_units), BF16),
+            jax.ShapeDtypeStruct((rows, hidden_units), BF16),
+            jax.ShapeDtypeStruct((rows, width), BF16),
+        ),
+        scratch_shapes=[pltpu.VMEM((rows, width), F32)],
+        cost_estimate=pl.CostEstimate(
+            flops=4 * rows * width * hidden_units,
+            bytes_accessed=36 << 20,
+            transcendentals=rows * hidden_units,
+        ),
+        name="expert",
+    )(routed, grad_act, weight)
+
+
+def first_grad_kernel(flip_ref, routed_ref, grad_ref, *refs):
+    step = pl.program_id(0)
+    half_steps = pl.num_programs(0) // 2
+    product_ref = refs[-1]
+    product_ref[...] = dot_tn(routed_ref[...], grad_ref[...]).astype(BF16)
+    owned = product_ref.shape[0] // 4
+
+    def piece(place):
+        row = pl.multiple_of((place ^ flip_ref[0]) * owned, owned)
+        return product_ref[pl.ds(row, owned), :]
+
+    keep_a, send_a, keep_b, send_b = refs[:-1]
+
+    @pl.when(step < half_steps)
+    def _():
+        for index, (kept, sent) in enumerate(((0, 1), (2, 3))):
+            keep_a[index] = piece(kept)
+            send_a[index] = piece(sent)
+
+    @pl.when(step >= half_steps)
+    def _():
+        for index, (kept, sent) in enumerate(((0, 2), (1, 3))):
+            keep_b[index] = piece(kept)
+            send_b[index] = piece(sent)
+
+
+def first_grad(flip, routed, grad, chunk=1024):
+    rows, width = routed.shape
+    columns = grad.shape[1]
+    steps = columns // chunk
+    shape = jax.ShapeDtypeStruct((2, width // 4, columns // 2), BF16)
+    block = (2, width // 4, chunk)
+    spec_a = pl.BlockSpec(block, lambda step: (0, 0, jnp.minimum(step, steps // 2 - 1)))
+    spec_b = pl.BlockSpec(block, lambda step: (0, 0, jnp.maximum(step - steps // 2, 0)))
+    return pl.pallas_call(
+        first_grad_kernel,
+        grid=(steps,),
+        in_specs=[
+            pl.BlockSpec(memory_space=pltpu.SMEM),
+            whole((rows, width)),
+            pl.BlockSpec((rows, chunk), lambda step: (0, step)),
+        ],
+        out_specs=(spec_a, spec_a, spec_b, spec_b),
+        out_shape=(shape,) * 4,
+        scratch_shapes=[pltpu.VMEM((width, chunk), BF16)],
+        cost_estimate=pl.CostEstimate(
+            flops=2 * rows * width * columns, bytes_accessed=18 << 20, transcendentals=0
+        ),
+        name="first_grad",
+    )(flip, routed, grad)
+
+
+def second_grad_kernel(flip_ref, act_ref, grad_ref, keep_a, send_a, keep_b, send_b):
+    step = pl.program_id(0)
+    product = dot_tn(act_ref[...], grad_ref[...]).astype(BF16)
+    half = product.shape[1] // 2
+
+    @pl.when(step == 0)
+    def _():
+        send_a[0] = product[:, :half]
+        send_b[0] = product[:, half:]
+
+    @pl.when(step == 1)
+    def _():
+        send_a[0] = product[:, :half]
+        keep_b[0] = product[:, half:]
+
+    @pl.when(step == 2)
+    def _():
+        keep_a[0] = product[:, :half]
+        send_b[0] = product[:, half:]
+
+    @pl.when(step == 3)
+    def _():
+        keep_a[0] = product[:, :half]
+        keep_b[0] = product[:, half:]
+
+
+def second_grad(flip, act, grad):
+    rows, width = grad.shape
+    owned = act.shape[1] // 4
+    shape = jax.ShapeDtypeStruct((2, owned, width // 2), BF16)
+    block = (1, owned, width // 2)
+
+    def spec(first_step):
+        return pl.BlockSpec(
+            block, lambda step, flip_ref: (1 - (step >= first_step).astype(jnp.int32), 0, 0)
+        )
+
+    return pl.pallas_call(
+        second_grad_kernel,
+        grid_spec=pltpu.PrefetchScalarGridSpec(
+            num_scalar_prefetch=1,
+            grid=(4,),
+            in_specs=[
+                pl.BlockSpec((rows, owned), lambda step, flip_ref: (0, place_of(step) ^ flip_ref[0])),
+                pl.BlockSpec((rows, width), lambda step, flip_ref: (0, 0)),
+            ],
+            out_specs=(spec(3), spec(1), spec(3), spec(2)),
+        ),
+        out_shape=(shape,) * 4,
+        cost_estimate=pl.CostEstimate(
+            flops=2 * rows * width * act.shape[1], bytes_accessed=18 << 20, transcendentals=0
+        ),
+        name="second_grad",
+    )(flip, act, grad)
+
+
+def place_of(step):
+    return jnp.where(step == 0, 3, jnp.where(step == 3, 0, step))
+
+
+def swap(values, axis, bits):
+    size = lax.axis_size(axis)
+    return lax.ppermute(values, axis, [(index, index ^ bits) for index in range(size)])
+
+
+def sum_over_copies(keep_a, send_a, keep_b, send_b):
+    got_a = swap(send_a, "rep", 1)
+    got_b = swap(send_b, "rep", 2)
+    more_a = swap(add_low(keep_a[1], got_a[1]), "rep", 2)
+    more_b = swap(add_low(keep_b[1], got_b[1]), "rep", 1)
+    half_a = keep_a[0].astype(F32) + got_a[0].astype(F32) + more_a.astype(F32)
+    half_b = keep_b[0].astype(F32) + got_b[0].astype(F32) + more_b.astype(F32)
+    return jnp.concatenate([half_a, half_b], 1)
+
+
+def add_low(left, right):
+    return (left.astype(F32) + right.astype(F32)).astype(BF16)
+
+
 def exchange(buffer, expert_count):
     shape = buffer.shape
     buffer = buffer.reshape(expert_count, shape[0] // expert_count, shape[1])
+    if expert_count <= 8:
+        pieces = [buffer[0]]
+        for bits in range(1, expert_count):
+            pieces.append(swap(buffer[bits], "ep", bits))
+        return jnp.concatenate(pieces, 0)
     buffer = lax.all_to_all(buffer, "ep", split_axis=0, concat_axis=0, tiled=True)
     return buffer.reshape(shape)
-
-
-def smooth_gate(values):
-    return jax.nn.gelu(values, approximate=True)
 
 
 def local(
@@ -469,12 +716,26 @@
     out_grad,
 ):
     tok_rows, width = tokens_in.shape
-    expert_count = expert_in.shape[0] * lax.axis_size("ep")
+    rep_size, ep_size = lax.axis_size("rep"), lax.axis_size("ep")
+    rep_bits, ep_bits = rep_size.bit_length() - 1, ep_size.bit_length() - 1
+    expert_count = expert_in.shape[0] * ep_size
     capacity = 2 * tok_rows // expert_count
     slot_total = expert_count * capacity
+    tile = width // (rep_size * ep_size)
+    paired = expert_count <= 8
     first_weight, second_weight = expert_in[0], expert_out[0]
-
-    slot_row, grad_buffer = route(token_ids, hash_table, out_grad, expert_count, capacity)
+    rep_index, ep_index = lax.axis_index("rep"), lax.axis_index("ep")
+    ep_flip = jnp.reshape(ep_index if paired else 0, (1,)).astype(jnp.int32)
+    rep_flip = jnp.reshape(rep_index, (1,)).astype(jnp.int32)
+    layout = tuple(reversed(range(rep_bits + ep_bits)))
+    spot = spread_bits(rep_index * ep_size + ep_index, layout)
+    spot = jnp.reshape(spot, (1,)).astype(jnp.int32)
+    if not paired:
+        layout, spot = tuple(range(rep_bits + ep_bits)), jnp.zeros((1,), jnp.int32)
+
+    slot_row, grad_buffer = route(
+        ep_flip, token_ids, hash_table, out_grad, expert_count, capacity
+    )
     grad_received = exchange(grad_buffer, expert_count)
     normed, query, key, value, probs, mixture, hidden, buffer = front(
         doc_lengths,
@@ -491,30 +752,17 @@
     received = exchange(buffer, expert_count)
     grad_act = jnp.einsum("sd,fd->sf", grad_received, second_weight, preferred_element_type=F32)
     grad_act = grad_act.astype(BF16)
-    pre_act = jnp.einsum("sd,df->sf", received, first_weight, preferred_element_type=F32)
-    gate_value, gate_pull = jax.vjp(smooth_gate, pre_act)
-    activation = gate_value.astype(BF16)
-    grad_pre = gate_pull(grad_act.astype(F32))[0].astype(BF16)
-    grad_routed = jnp.einsum(
-        "sf,df->sd", grad_pre, first_weight, preferred_element_type=F32
-    ).astype(BF16)
+    act, grad_pre, grad_routed = expert(received, grad_act, first_weight)
     grad_back = exchange(grad_routed, expert_count)
-    grad_second = jnp.einsum(
-        "sf,sd->fd", activation, grad_received, preferred_element_type=F32
-    ).astype(BF16)
-    grad_first = jnp.einsum("sd,sf->df", received, grad_pre, preferred_element_type=F32).astype(
-        BF16
-    )
-    summed_second = lax.psum_scatter(grad_second, "rep", scatter_dimension=0, tiled=True)
-    summed_first = lax.psum_scatter(grad_first, "rep", scatter_dimension=0, tiled=True)
-    result = jnp.einsum(
-        "sf,fd->sd", activation, second_weight, preferred_element_type=F32
-    ).astype(BF16)
-    grad_back, grad_second, grad_first, result = lax.optimization_barrier(
-        (grad_back, grad_second, grad_first, result)
-    )
+    summed_second = sum_over_copies(*second_grad(rep_flip, act, grad_received))
+    summed_first = sum_over_copies(*first_grad(rep_flip, received, grad_pre))
+    result = jnp.einsum("sf,fd->sd", act, second_weight, preferred_element_type=F32).astype(BF16)
+    grad_back, result = lax.optimization_barrier((grad_back, result))
     returned = exchange(result, expert_count)
-    dense, small, grad_in = back(
+    dense, grad_in = back(
+        tile,
+        layout,
+        spot,
         grad_back,
         slot_row,
         hidden,
@@ -531,10 +779,16 @@
         tokens_in,
         gain_one,
     )
-    columns = jnp.pad(small, ((0, LANES - small.shape[0]), (0, 0))).T.astype(BF16)
-    dense = jnp.concatenate([dense, columns], 1)
-    dense = lax.psum_scatter(dense, "rep", scatter_dimension=0, tiled=True)
-    dense = lax.psum_scatter(dense, "ep", scatter_dimension=0, tiled=True).astype(F32)
+    if paired:
+        for bits in [("ep", 1 << bit) for bit in range(ep_bits)] + [
+            ("rep", 1 << bit) for bit in range(rep_bits)
+        ]:
+            half = dense.shape[0] // 2
+            dense = add_low(dense[:half], swap(dense[half:], *bits))
+    else:
+        dense = lax.psum_scatter(dense, "rep", scatter_dimension=0, tiled=True)
+        dense = lax.psum_scatter(dense, "ep", scatter_dimension=0, tiled=True)
+    dense = dense.astype(F32)
     block_out = finish(hidden, slot_row, returned)
     return (
         block_out,
@@ -545,8 +799,8 @@
         dense[:, 4 * width + 3],
         dense[:, 4 * width],
         dense[:, 4 * width + 1],
-        summed_first.astype(F32)[None],
-        summed_second.astype(F32)[None],
+        summed_first[None],
+        summed_second[None],
     )
 
 

time: 623 us -> 511 us (0.82)
  waiting for transfers between devices: 339 us -> 228 us
  matrix products: 104 us -> 29.6 us
  Pallas kernels: 68.7 us -> 128 us
  blocking collectives: 55.4 us -> 0 us
  starting transfers between devices: 12.4 us -> 52.5 us
  local copies, waits for them, and re-layouts: 6.79 us -> 36 us
  between operations: 14.3 us -> 1.53 us
  other arithmetic: 17.4 us -> 25.8 us
    reduce_scatter x4 -> x0, waiting for transfers between devices: 285 us -> none  [the longest x1 85.3 us: local(): lax.psum_scatter(grad_first, 'rep', scatter_dimension=0, tiled=True)]
    ppermute x0 -> x41, waiting for transfers between devices: none -> 228 us  [swap(): lax.ppermute(values, axis, [(index, index ^ bits) for index in range(size)])]
    dot_general x5 -> x1, matrix products: 78.9 us -> 14.6 us  [local(): jnp.einsum('sf,fd->sd', act, second_weight, preferred_element_type=F32)]
    pallas_call x2 -> x5, Pallas kernels: 41.7 us -> 101 us  [the longest x1 37.7 us: back(): pl.pallas_call(functools.partial(back_kernel, head_size, tile, layout), g...]
    all_to_all x1 -> x0, blocking collectives: 55.4 us -> none  [exchange(): lax.all_to_all(buffer, 'ep', split_axis=0, concat_axis=0, tiled=True)]
    ppermute x0 -> x41, starting transfers between devices: none -> 52.5 us  [swap(): lax.ppermute(values, axis, [(index, index ^ bits) for index in range(size)])]
    all_to_all x3 -> x0, waiting for transfers between devices: 51.6 us -> none  [exchange(): lax.all_to_all(buffer, 'ep', split_axis=0, concat_axis=0, tiled=True)]
    slice x0 -> x9, local copies, waits for them, and re-layouts: none -> 15.8 us  [the longest x4 9.35 us: exchange(): pieces.append(swap(buffer[bits], 'ep', bits))]
  transfers between devices with their start and end apart: 7 -> 41, of which waited for: 6 -> 18; matrix products, arithmetic and copies ran while one was open for 9% -> 15% of each run, Pallas kernels for 1% -> 11%
where the time goes in v3:
time: 511 us; the launch traced here: 502 us
  waiting for transfers between devices  228 us (45%)
  Pallas kernels  128 us (25%)
  starting transfers between devices  52.5 us (10%)
  local copies, waits for them, and re-layouts  36 us (7%)
  matrix products  29.6 us (6%)
  other arithmetic  25.8 us (5%)
    ppermute x41, waiting for transfers between devices, swap(): lax.ppermute(values, axis, [(index, index ^ bits) for index in range(size)])  228 us
    ppermute x41, starting transfers between devices, swap(): lax.ppermute(values, axis, [(index, index ^ bits) for index in range(size)])  52.5 us
    pallas_call x1, Pallas kernels, back(): pl.pallas_call(functools.partial(back_kernel, head_size, tile, layout), g...  37.7 us
    pallas_call x1, Pallas kernels, expert(): pl.pallas_call(functools.partial(expert_kernel, tile), grid=(hidden_units...  29.7 us
    pallas_call x1, Pallas kernels, front(): pl.pallas_call(functools.partial(front_kernel, slot_total, head_size), gr...  22.5 us
    unnamed x46, local copies, waits for them, and re-layouts  16.4 us
    pallas_call x1, Pallas kernels, second_grad(): pl.pallas_call(second_grad_kernel, grid_spec=pltpu.PrefetchScalarGridSpec...  15 us
    dot_general x1, matrix products, local(): jnp.einsum('sd,fd->sf', grad_received, second_weight, preferred_element_t...  15 us
  transfers between devices with their start and end apart: 41, of which 18 were waited for; matrix products, arithmetic and copies ran while one was open for 15% of the time, Pallas kernels for 11%

profile of v3, /device:TPU:0, one launch (start us, length us, event | category | flops | bytes accessed | tf_op | source)
XLA Modules:
  0.0 501.5 jit_solution(8120059371925562828)
XLA Ops:
  0.6 4.2 route.1
  4.8 2.6 fusion.17
  7.4 4.5 collective-permute-start.13
  12.5 1.7 collective-permute-start.8
  14.4 22.5 %front.1 = (bf16[512,1024]{1,0:T(8,128)(2,1)}, bf16[512,1024]{1,0:T(8,128)(2,1)}, bf16[512,1024]{1,0:T(8,128)(2,1)}, bf16[512,1024]{1,0:T(8,128)(2,1)}, bf16[16,...) custom-call(s32[1,4]{1,0:T(1,128)} %lengths_ref.1, ...), custom_call_target="tpu_custom_call" | custom-call | flops 14000000000 | bytes 31457280 | tf_op jit(solution)/shard_map/front/pallas_call | solution.py:206
  36.9 2.5 fusion.18
  39.4 2.1 collective-permute-start.10
  45.4 3.4 collective-permute-start.6
  50.5 15.8 %collective-permute-done.10 = bf16[128,1024]{1,0:T(8,128)(2,1)S(1)} collective-permute-done((bf16[128,1024]{1,0:T(8,128)(2,1)S(1)}, bf16[128,1024]{1,0:T(8,128)(2,1)S(1)}, u32[]{:S(2)}, u32[]{:S(2)}) %collective-permute-start.10) | collective-permute-done | bytes 262176 | tf_op jit(solution)/shard_map/ppermute | solution.py:674
  66.3 2.5 collective-permute-start.5
  69.5 6.9 %collective-permute-done.11 = bf16[128,1024]{1,0:T(8,128)(2,1)S(1)} collective-permute-done((bf16[128,1024]{1,0:T(8,128)(2,1)S(1)}, bf16[128,1024]{1,0:T(8,128)(2,1)S(1)}, u32[]{:S(2)}, u32[]{:S(2)}) %collective-permute-start.11) | collective-permute-done | bytes 262176 | tf_op jit(solution)/shard_map/ppermute | solution.py:674
  77.5 2.2 collective-permute-start.1
  83.1 15.0 %fusion.4.grad_act_ref = bf16[1024,4096]{1,0:T(8,128)(2,1)} fusion(bf16[1024,1024]{1,0:T(8,128)(2,1)} %constant_dynamic-update-slice_fusion.7.grad_ref, bf16[1,4096,1024]{2,1,0:T(8,128)(2,1)} %param.24), kind=kOutput, calls=%fused_computation.5 | convolution fusion | flops 8594128896 | bytes 18874368 | tf_op jit(solution)/shard_map/sd,fd->sf/dot_general | solution.py:753
  100.9 18.1 %collective-permute-done.3 = bf16[128,1024]{1,0:T(8,128)(2,1)S(1)} collective-permute-done((bf16[128,1024]{1,0:T(8,128)(2,1)S(1)}, bf16[128,1024]{1,0:T(8,128)(2,1)S(1)}, u32[]{:S(2)}, u32[]{:S(2)}) %collective-permute-start.3) | collective-permute-done | bytes 262176 | tf_op jit(solution)/shard_map/ppermute | solution.py:674
  119.0 5.3 %collective-permute-done.4 = bf16[128,1024]{1,0:T(8,128)(2,1)S(1)} collective-permute-done((bf16[128,1024]{1,0:T(8,128)(2,1)S(1)}, bf16[128,1024]{1,0:T(8,128)(2,1)S(1)}, u32[]{:S(2)}, u32[]{:S(2)}) %collective-permute-start.4) | collective-permute-done | bytes 262176 | tf_op jit(solution)/shard_map/ppermute | solution.py:674
  125.8 29.7 %expert.1 = (bf16[1024,4096]{1,0:T(8,128)(2,1)}, bf16[1024,4096]{1,0:T(8,128)(2,1)}, bf16[1024,1024]{1,0:T(8,128)(2,1)}) custom-call(bf16[1024,1024]{1,0:T(8,128)(2,1)} %copy-done.7, bf16[1024,4096]{1,0:T(8,128)(2,1)} %fusion.4.grad_act_ref, bf16[1024,4096]{1,0:T(8,128)(2,1)} %bitcast.43), custom_call_target="tpu_custom_call" | custom-call | flops 17179869184 | bytes 37748736 | tf_op jit(solution)/shard_map/expert/pallas_call | solution.py:536
  157.1 2.3 collective-permute-start.20
  160.8 1.7 collective-permute-start.15
  162.6 14.6 %fusion.7 = bf16[1024,1024]{1,0:T(8,128)(2,1)} fusion(bf16[1024,4096]{1,0:T(8,128)(2,1)} %get-tuple-element.40.act_ref, bf16[1,4096,1024]{2,1,0:T(8,128)(2,1)} %param.24), kind=kOutput, calls=%fused_computation.18 | convolution fusion | flops 8590983168 | bytes 18874368 | tf_op jit(solution)/shard_map/sf,fd->sd/dot_general | solution.py:759
  178.6 8.8 %collective-permute-done.15 = bf16[128,1024]{1,0:T(8,128)(2,1)S(1)} collective-permute-done((bf16[128,1024]{1,0:T(8,128)(2,1)S(1)}, bf16[128,1024]{1,0:T(8,128)(2,1)S(1)}, u32[]{:S(2)}, u32[]{:S(2)}) %collective-permute-start.15) | collective-permute-done | bytes 262176 | tf_op jit(solution)/shard_map/ppermute | solution.py:674
  188.3 10.6 %collective-permute-done.17 = bf16[128,1024]{1,0:T(8,128)(2,1)S(1)} collective-permute-done((bf16[128,1024]{1,0:T(8,128)(2,1)S(1)}, bf16[128,1024]{1,0:T(8,128)(2,1)S(1)}, u32[]{:S(2)}, u32[]{:S(2)}) %collective-permute-start.17) | collective-permute-done | bytes 262176 | tf_op jit(solution)/shard_map/ppermute | solution.py:674
  199.0 5.2 %collective-permute-done.18 = bf16[128,1024]{1,0:T(8,128)(2,1)S(1)} collective-permute-done((bf16[128,1024]{1,0:T(8,128)(2,1)S(1)}, bf16[128,1024]{1,0:T(8,128)(2,1)S(1)}, u32[]{:S(2)}, u32[]{:S(2)}) %collective-permute-start.18) | collective-permute-done | bytes 262176 | tf_op jit(solution)/shard_map/ppermute | solution.py:674
  205.6 37.7 %back.1 = (bf16[1024,4224]{1,0:T(8,128)(2,1)}, f32[512,1024]{1,0:T(8,128)}) custom-call(s32[1]{0:T(128)} %bitcast.9.spot_ref, bf16[1024,1024]{1,0:T(8,128)(2,1)} %copy-done.8, s32[1,512]{1,0:T(1,128)} %get-tuple-element.35.slot_ref, f32[512,1024]{1,0:T(8,128)} %get-tuple-element.36.hidden_ref, f32[1,1024]{1,0:T(1,128)} %bitcast.50, ...), custom_call_target="tpu_custom_call" | custom-call | flops 24000000000 | bytes 52428800 | tf_op jit(solution)/shard_map/back/pallas_call | solution.py:423
  243.3 4.6 slice.257
  248.1 15.0 %second_grad.1 = (bf16[2,1024,512]{2,1,0:T(8,128)(2,1)}, bf16[2,1024,512]{2,1,0:T(8,128)(2,1)}, bf16[2,1024,512]{2,1,0:T(8,128)(2,1)}, bf16[2,1024,512]{2,1,0:T(8,128)(2,1)}) custom-call(s32[1]{0:T(128)} %bitcast.10.flip_ref, bf16[1024,4096]{1,0:T(8,128)(2,1)} %get-tuple-element.40.act_ref, bf16[1024,1024]{1,0:T(8,128)(2,1)} %constant_dynamic-update-slice_fusion.7.grad_ref), custom_call_target="tpu_custom_call" | custom-call | flops 8589934592 | bytes 18874368 | tf_op jit(solution)/shard_map/second_grad/pallas_call | solution.py:649
  263.1 2.6 fusion.15
  265.6 2.0 collective-permute-start.22
  267.7 14.5 %first_grad.1 = (bf16[2,256,2048]{2,1,0:T(8,128)(2,1)}, bf16[2,256,2048]{2,1,0:T(8,128)(2,1)}, bf16[2,256,2048]{2,1,0:T(8,128)(2,1)}, bf16[2,256,2048]{2,1,0:T(8,128)(2,1)}) custom-call(s32[1]{0:T(128)} %bitcast.10.flip_ref, bf16[1024,1024]{1,0:T(8,128)(2,1)} %copy-done.7, bf16[1024,4096]{1,0:T(8,128)(2,1)} %get-tuple-element.51.grad_ref), custom_call_target="tpu_custom_call" | custom-call | flops 8589934592 | bytes 18874368 | tf_op jit(solution)/shard_map/first_grad/pallas_call | solution.py:594
  285.0 2.2 collective-permute-start.25
  290.6 18.8 %collective-permute-done.24 = bf16[128,1024]{1,0:T(8,128)(2,1)S(1)} collective-permute-done((bf16[128,1024]{1,0:T(8,128)(2,1)S(1)}, bf16[128,1024]{1,0:T(8,128)(2,1)S(1)}, u32[]{:S(2)}, u32[]{:S(2)}) %collective-permute-start.24) | collective-permute-done | bytes 262176 | tf_op jit(solution)/shard_map/ppermute | solution.py:674
  310.9 3.9 collective-permute-done.25
  318.0 4.5 add_convert_fusion
  325.2 2.1 collective-permute-done.27
  327.3 6.1 %collective-permute-start.29 = (bf16[256,4224]{1,0:T(8,128)(2,1)}, bf16[256,4224]{1,0:T(8,128)(2,1)}, u32[]{:S(2)}, u32[]{:S(2)}) collective-permute-start(bf16[256,4224]{1,0:T(8,128)(2,1)} %slice.289), channel_id=1, source_target_pairs={{0,2},{1,3},{2,0},{3,1},{4,6},{5,7},{6,4},{7,5},{8,10},{9,11},{10,... | collective-permute-start | bytes 6488072 | tf_op jit(solution)/shard_map/ppermute | solution.py:674
  334.7 4.5 finish.1
  339.2 2.0 fusion.12
  341.8 16.4 %collective-permute-done.39 = bf16[2,1024,512]{2,1,0:T(8,128)(2,1)} collective-permute-done((bf16[2,1024,512]{2,1,0:T(8,128)(2,1)}, bf16[2,1024,512]{2,1,0:T(8,128)(2,1)}, u32[]{:S(2)}, u32[]{:S(2)}) %collective-permute-start.39) | collective-permute-done | bytes 2097184 | tf_op jit(solution)/shard_map/ppermute | solution.py:674
  360.5 15.5 %collective-permute-done.33 = bf16[2,256,2048]{2,1,0:T(8,128)(2,1)} collective-permute-done((bf16[2,256,2048]{2,1,0:T(8,128)(2,1)}, bf16[2,256,2048]{2,1,0:T(8,128)(2,1)}, u32[]{:S(2)}, u32[]{:S(2)}) %collective-permute-start.33) | collective-permute-done | bytes 2097184 | tf_op jit(solution)/shard_map/ppermute | solution.py:674
  375.9 1.8 fusion.10
  379.3 23.8 %collective-permute-done.35 = bf16[2,256,2048]{2,1,0:T(8,128)(2,1)} collective-permute-done((bf16[2,256,2048]{2,1,0:T(8,128)(2,1)}, bf16[2,256,2048]{2,1,0:T(8,128)(2,1)}, u32[]{:S(2)}, u32[]{:S(2)}) %collective-permute-start.35) | collective-permute-done | bytes 2097184 | tf_op jit(solution)/shard_map/ppermute | solution.py:674
  405.4 20.1 %collective-permute-done.38 = bf16[1024,512]{1,0:T(8,128)(2,1)S(1)} collective-permute-done((bf16[1024,512]{1,0:T(8,128)(2,1)S(1)}, bf16[1024,512]{1,0:T(8,128)(2,1)S(1)}, u32[]{:S(2)}, u32[]{:S(2)}) %collective-permute-start.38) | collective-permute-done | bytes 1048608 | tf_op jit(solution)/shard_map/ppermute | solution.py:674
  427.2 2.2 add_convert_fusion.1
  429.5 17.4 %collective-permute-done.34 = bf16[256,2048]{1,0:T(8,128)(2,1)S(1)} collective-permute-done((bf16[256,2048]{1,0:T(8,128)(2,1)S(1)}, bf16[256,2048]{1,0:T(8,128)(2,1)S(1)}, u32[]{:S(2)}, u32[]{:S(2)}) %collective-permute-start.34) | collective-permute-done | bytes 1048608 | tf_op jit(solution)/shard_map/ppermute | solution.py:674
  450.4 26.1 %collective-permute-done.30 = bf16[128,4224]{1,0:T(8,128)(2,1)S(1)} collective-permute-done((bf16[128,4224]{1,0:T(8,128)(2,1)S(1)}, bf16[128,4224]{1,0:T(8,128)(2,1)S(1)}, u32[]{:S(2)}, u32[]{:S(2)}) %collective-permute-start.30) | collective-permute-done | bytes 1081376 | tf_op jit(solution)/shard_map/ppermute | solution.py:674
  477.4 2.5 maximum_bitcast_fusion
  479.9 11.2 %collective-permute-done.31 = bf16[64,4224]{1,0:T(8,128)(2,1)S(1)} collective-permute-done((bf16[64,4224]{1,0:T(8,128)(2,1)S(1)}, bf16[64,4224]{1,0:T(8,128)(2,1)S(1)}, u32[]{:S(2)}, u32[]{:S(2)}) %collective-permute-start.31) | collective-permute-done | bytes 540704 | tf_op jit(solution)/shard_map/ppermute | solution.py:674
  494.4 2.4 maximum_bitcast_fusion.1
  496.9 2.0 collective-permute-done.32
  (121 shorter events, 56.0 us)
Async XLA Ops:
  7.4 74.0 %collective-permute-start.13 = (bf16[128,1024]{1,0:T(8,128)(2,1)S(1)}, bf16[128,1024]{1,0:T(8,128)(2,1)}, u32[]{:S(2)}, u32[]{:S(2)}) collective-permute-start(bf16[128,1024]{1,0:T(8,128)(2,1)S(1)} %get-tuple-element.80), channel_id=1, source_target_pairs={{0,7},{1,6},{2,5},{3,4},{4,3},{5,2},{6,1},{7,0},{8,15},{9,14},{10,... | collective-permute-start | bytes 786440 | tf_op jit(solution)/shard_map/ppermute | solution.py:674
  11.9 65.6 %collective-permute-start.12 = (bf16[128,1024]{1,0:T(8,128)(2,1)S(1)}, bf16[128,1024]{1,0:T(8,128)(2,1)}, u32[]{:S(2)}, u32[]{:S(2)}) collective-permute-start(bf16[128,1024]{1,0:T(8,128)(2,1)S(1)} %get-tuple-element.81), channel_id=1, source_target_pairs={{0,6},{1,7},{2,4},{3,5},{4,2},{5,3},{6,0},{7,1},{8,14},{9,15},{10,... | collective-permute-start | bytes 786440 | tf_op jit(solution)/shard_map/ppermute | solution.py:674
  12.5 32.9 %collective-permute-start.9 = (bf16[128,1024]{1,0:T(8,128)(2,1)S(1)}, bf16[128,1024]{1,0:T(8,128)(2,1)}, u32[]{:S(2)}, u32[]{:S(2)}) collective-permute-start(bf16[128,1024]{1,0:T(8,128)(2,1)S(1)} %get-tuple-element.84), channel_id=1, source_target_pairs={{0,3},{1,2},{2,1},{3,0},{4,7},{5,6},{6,5},{7,4},{8,11},{9,10},{10,... | collective-permute-start | bytes 786440 | tf_op jit(solution)/shard_map/ppermute | solution.py:674
  12.5 30.6 %collective-permute-start.8 = (bf16[128,1024]{1,0:T(8,128)(2,1)S(1)}, bf16[128,1024]{1,0:T(8,128)(2,1)}, u32[]{:S(2)}, u32[]{:S(2)}) collective-permute-start(bf16[128,1024]{1,0:T(8,128)(2,1)S(1)} %get-tuple-element.85), channel_id=1, source_target_pairs={{0,2},{1,3},{2,0},{3,1},{4,6},{5,7},{6,4},{7,5},{8,10},{9,11},{10,... | collective-permute-start | bytes 786440 | tf_op jit(solution)/shard_map/ppermute | solution.py:674
  14.2 25.1 %collective-permute-start.7 = (bf16[128,1024]{1,0:T(8,128)(2,1)}, bf16[128,1024]{1,0:T(8,128)(2,1)}, u32[]{:S(2)}, u32[]{:S(2)}) collective-permute-start(bf16[128,1024]{1,0:T(8,128)(2,1)} %get-tuple-element.86), channel_id=1, source_target_pairs={{0,1},{1,0},{2,3},{3,2},{4,5},{5,4},{6,7},{7,6},{8,9},{9,8},{10,11... | collective-permute-start | bytes 786440 | tf_op jit(solution)/shard_map/ppermute | solution.py:674
  39.4 26.9 %collective-permute-start.10 = (bf16[128,1024]{1,0:T(8,128)(2,1)S(1)}, bf16[128,1024]{1,0:T(8,128)(2,1)S(1)}, u32[]{:S(2)}, u32[]{:S(2)}) collective-permute-start(bf16[128,1024]{1,0:T(8,128)(2,1)S(1)} %get-tuple-element.83), channel_id=1, source_target_pairs={{0,4},{1,5},{2,6},{3,7},{4,0},{5,1},{6,2},{7,3},{8,12},{9,13},{10,... | collective-permute-start | bytes 786440 | tf_op jit(solution)/shard_map/ppermute | solution.py:674
  43.1 33.3 %collective-permute-start.11 = (bf16[128,1024]{1,0:T(8,128)(2,1)S(1)}, bf16[128,1024]{1,0:T(8,128)(2,1)S(1)}, u32[]{:S(2)}, u32[]{:S(2)}) collective-permute-start(bf16[128,1024]{1,0:T(8,128)(2,1)S(1)} %get-tuple-element.82), channel_id=1, source_target_pairs={{0,5},{1,4},{2,7},{3,6},{4,1},{5,0},{6,3},{7,2},{8,13},{9,12},{10,... | collective-permute-start | bytes 786440 | tf_op jit(solution)/shard_map/ppermute | solution.py:674
  45.4 79.0 %collective-permute-start.6 = (bf16[128,1024]{1,0:T(8,128)(2,1)S(1)}, bf16[128,1024]{1,0:T(8,128)(2,1)S(1)}, u32[]{:S(2)}, u32[]{:S(2)}) collective-permute-start(bf16[128,1024]{1,0:T(8,128)(2,1)S(1)} %get-tuple-element.88), channel_id=1, source_target_pairs={{0,7},{1,6},{2,5},{3,4},{4,3},{5,2},{6,1},{7,0},{8,15},{9,14},{10,... | collective-permute-start | bytes 786440 | tf_op jit(solution)/shard_map/ppermute | solution.py:674
  66.3 58.1 %collective-permute-start.5 = (bf16[128,1024]{1,0:T(8,128)(2,1)S(1)}, bf16[128,1024]{1,0:T(8,128)(2,1)S(1)}, u32[]{:S(2)}, u32[]{:S(2)}) collective-permute-start(bf16[128,1024]{1,0:T(8,128)(2,1)S(1)} %get-tuple-element.89), channel_id=1, source_target_pairs={{0,6},{1,7},{2,4},{3,5},{4,2},{5,3},{6,0},{7,1},{8,14},{9,15},{10,... | collective-permute-start | bytes 786440 | tf_op jit(solution)/shard_map/ppermute | solution.py:674
  76.4 24.5 %collective-permute-start.2 = (bf16[128,1024]{1,0:T(8,128)(2,1)S(1)}, bf16[128,1024]{1,0:T(8,128)(2,1)S(1)}, u32[]{:S(2)}, u32[]{:S(2)}) collective-permute-start(bf16[128,1024]{1,0:T(8,128)(2,1)S(1)} %get-tuple-element.92), channel_id=1, source_target_pairs={{0,3},{1,2},{2,1},{3,0},{4,7},{5,6},{6,5},{7,4},{8,11},{9,10},{10,... | collective-permute-start | bytes 786440 | tf_op jit(solution)/shard_map/ppermute | solution.py:674
  77.5 22.1 %collective-permute-start.1 = (bf16[128,1024]{1,0:T(8,128)(2,1)S(1)}, bf16[128,1024]{1,0:T(8,128)(2,1)S(1)}, u32[]{:S(2)}, u32[]{:S(2)}) collective-permute-start(bf16[128,1024]{1,0:T(8,128)(2,1)S(1)} %get-tuple-element.93), channel_id=1, source_target_pairs={{0,2},{1,3},{2,0},{3,1},{4,6},{5,7},{6,4},{7,5},{8,10},{9,11},{10,... | collective-permute-start | bytes 786440 | tf_op jit(solution)/shard_map/ppermute | solution.py:674
  81.4 16.6 %collective-permute-start = (bf16[128,1024]{1,0:T(8,128)(2,1)S(1)}, bf16[128,1024]{1,0:T(8,128)(2,1)S(1)}, u32[]{:S(2)}, u32[]{:S(2)}) collective-permute-start(bf16[128,1024]{1,0:T(8,128)(2,1)S(1)} %get-tuple-element.94), channel_id=1, source_target_pairs={{0,1},{1,0},{2,3},{3,2},{4,5},{5,4},{6,7},{7,6},{8,9},{9,8},{10,11... | collective-permute-start | bytes 786440 | tf_op jit(solution)/shard_map/ppermute | solution.py:674
  83.1 16.6 %copy-start.6 = (bf16[1024,1024]{1,0:T(8,128)(2,1)S(1)}, bf16[1024,1024]{1,0:T(8,128)(2,1)}, u32[]{:S(2)}) copy-start(bf16[1024,1024]{1,0:T(8,128)(2,1)} %get-tuple-element.95) | copy-start | bytes 6291460
  98.0 21.0 %collective-permute-start.3 = (bf16[128,1024]{1,0:T(8,128)(2,1)S(1)}, bf16[128,1024]{1,0:T(8,128)(2,1)S(1)}, u32[]{:S(2)}, u32[]{:S(2)}) collective-permute-start(bf16[128,1024]{1,0:T(8,128)(2,1)S(1)} %get-tuple-element.91), channel_id=1, source_target_pairs={{0,4},{1,5},{2,6},{3,7},{4,0},{5,1},{6,2},{7,3},{8,12},{9,13},{10,... | collective-permute-start | bytes 786440 | tf_op jit(solution)/shard_map/ppermute | solution.py:674
  99.7 24.7 %collective-permute-start.4 = (bf16[128,1024]{1,0:T(8,128)(2,1)S(1)}, bf16[128,1024]{1,0:T(8,128)(2,1)S(1)}, u32[]{:S(2)}, u32[]{:S(2)}) collective-permute-start(bf16[128,1024]{1,0:T(8,128)(2,1)S(1)} %get-tuple-element.90), channel_id=1, source_target_pairs={{0,5},{1,4},{2,7},{3,6},{4,1},{5,0},{6,3},{7,2},{8,13},{9,12},{10,... | collective-permute-start | bytes 786440 | tf_op jit(solution)/shard_map/ppermute | solution.py:674
  157.1 47.1 %collective-permute-start.20 = (bf16[128,1024]{1,0:T(8,128)(2,1)S(1)}, bf16[128,1024]{1,0:T(8,128)(2,1)S(1)}, u32[]{:S(2)}, u32[]{:S(2)}) collective-permute-start(bf16[128,1024]{1,0:T(8,128)(2,1)S(1)} %get-tuple-element.72), channel_id=1, source_target_pairs={{0,7},{1,6},{2,5},{3,4},{4,3},{5,2},{6,1},{7,0},{8,15},{9,14},{10,... | collective-permute-start | bytes 786440 | tf_op jit(solution)/shard_map/ppermute | solution.py:674
  159.4 44.8 %collective-permute-start.19 = (bf16[128,1024]{1,0:T(8,128)(2,1)S(1)}, bf16[128,1024]{1,0:T(8,128)(2,1)S(1)}, u32[]{:S(2)}, u32[]{:S(2)}) collective-permute-start(bf16[128,1024]{1,0:T(8,128)(2,1)S(1)} %get-tuple-element.73), channel_id=1, source_target_pairs={{0,6},{1,7},{2,4},{3,5},{4,2},{5,3},{6,0},{7,1},{8,14},{9,15},{10,... | collective-permute-start | bytes 786440 | tf_op jit(solution)/shard_map/ppermute | solution.py:674
  160.8 27.5 %collective-permute-start.16 = (bf16[128,1024]{1,0:T(8,128)(2,1)S(1)}, bf16[128,1024]{1,0:T(8,128)(2,1)S(1)}, u32[]{:S(2)}, u32[]{:S(2)}) collective-permute-start(bf16[128,1024]{1,0:T(8,128)(2,1)S(1)} %get-tuple-element.76), channel_id=1, source_target_pairs={{0,3},{1,2},{2,1},{3,0},{4,7},{5,6},{6,5},{7,4},{8,11},{9,10},{10,... | collective-permute-start | bytes 786440 | tf_op jit(solution)/shard_map/ppermute | solution.py:674
  160.8 26.6 %collective-permute-start.15 = (bf16[128,1024]{1,0:T(8,128)(2,1)S(1)}, bf16[128,1024]{1,0:T(8,128)(2,1)S(1)}, u32[]{:S(2)}, u32[]{:S(2)}) collective-permute-start(bf16[128,1024]{1,0:T(8,128)(2,1)S(1)} %get-tuple-element.77), channel_id=1, source_target_pairs={{0,2},{1,3},{2,0},{3,1},{4,6},{5,7},{6,4},{7,5},{8,10},{9,11},{10,... | collective-permute-start | bytes 786440 | tf_op jit(solution)/shard_map/ppermute | solution.py:674
  162.5 14.8 %collective-permute-start.14 = (bf16[128,1024]{1,0:T(8,128)(2,1)S(1)}, bf16[128,1024]{1,0:T(8,128)(2,1)S(1)}, u32[]{:S(2)}, u32[]{:S(2)}) collective-permute-start(bf16[128,1024]{1,0:T(8,128)(2,1)S(1)} %get-tuple-element.78), channel_id=1, source_target_pairs={{0,1},{1,0},{2,3},{3,2},{4,5},{5,4},{6,7},{7,6},{8,9},{9,8},{10,11... | collective-permute-start | bytes 786440 | tf_op jit(solution)/shard_map/ppermute | solution.py:674
  177.3 21.7 %collective-permute-start.17 = (bf16[128,1024]{1,0:T(8,128)(2,1)S(1)}, bf16[128,1024]{1,0:T(8,128)(2,1)S(1)}, u32[]{:S(2)}, u32[]{:S(2)}) collective-permute-start(bf16[128,1024]{1,0:T(8,128)(2,1)S(1)} %get-tuple-element.75), channel_id=1, source_target_pairs={{0,4},{1,5},{2,6},{3,7},{4,0},{5,1},{6,2},{7,3},{8,12},{9,13},{10,... | collective-permute-start | bytes 786440 | tf_op jit(solution)/shard_map/ppermute | solution.py:674
  187.3 16.8 %collective-permute-start.18 = (bf16[128,1024]{1,0:T(8,128)(2,1)S(1)}, bf16[128,1024]{1,0:T(8,128)(2,1)S(1)}, u32[]{:S(2)}, u32[]{:S(2)}) collective-permute-start(bf16[128,1024]{1,0:T(8,128)(2,1)S(1)} %get-tuple-element.74), channel_id=1, source_target_pairs={{0,5},{1,4},{2,7},{3,6},{4,1},{5,0},{6,3},{7,2},{8,13},{9,12},{10,... | collective-permute-start | bytes 786440 | tf_op jit(solution)/shard_map/ppermute | solution.py:674
  247.9 69.1 %collective-permute-start.28 = (bf16[512,4224]{1,0:T(8,128)(2,1)}, bf16[512,4224]{1,0:T(8,128)(2,1)}, u32[]{:S(2)}, u32[]{:S(2)}) collective-permute-start(bf16[512,4224]{1,0:T(8,128)(2,1)} %slice.257), channel_id=1, source_target_pairs={{0,1},{1,0},{2,3},{3,2},{4,5},{5,4},{6,7},{7,6},{8,9},{9,8},{10,11... | collective-permute-start | bytes 12976136 | tf_op jit(solution)/shard_map/ppermute | solution.py:674
  265.6 22.5 %collective-permute-start.23 = (bf16[128,1024]{1,0:T(8,128)(2,1)S(1)}, bf16[128,1024]{1,0:T(8,128)(2,1)}, u32[]{:S(2)}, u32[]{:S(2)}) collective-permute-start(bf16[128,1024]{1,0:T(8,128)(2,1)S(1)} %get-tuple-element.68), channel_id=1, source_target_pairs={{0,3},{1,2},{2,1},{3,0},{4,7},{5,6},{6,5},{7,4},{8,11},{9,10},{10,... | collective-permute-start | bytes 786440 | tf_op jit(solution)/shard_map/ppermute | solution.py:674
  265.6 19.3 %collective-permute-start.22 = (bf16[128,1024]{1,0:T(8,128)(2,1)}, bf16[128,1024]{1,0:T(8,128)(2,1)}, u32[]{:S(2)}, u32[]{:S(2)}) collective-permute-start(bf16[128,1024]{1,0:T(8,128)(2,1)} %get-tuple-element.69), channel_id=1, source_target_pairs={{0,2},{1,3},{2,0},{3,1},{4,6},{5,7},{6,4},{7,5},{8,10},{9,11},{10,... | collective-permute-start | bytes 786440 | tf_op jit(solution)/shard_map/ppermute | solution.py:674
  267.7 16.0 %collective-permute-start.21 = (bf16[128,1024]{1,0:T(8,128)(2,1)}, bf16[128,1024]{1,0:T(8,128)(2,1)}, u32[]{:S(2)}, u32[]{:S(2)}) collective-permute-start(bf16[128,1024]{1,0:T(8,128)(2,1)} %get-tuple-element.70), channel_id=1, source_target_pairs={{0,1},{1,0},{2,3},{3,2},{4,5},{5,4},{6,7},{7,6},{8,9},{9,8},{10,11... | collective-permute-start | bytes 786440 | tf_op jit(solution)/shard_map/ppermute | solution.py:674
  282.2 57.1 %collective-permute-start.37 = (bf16[2,1024,512]{2,1,0:T(8,128)(2,1)}, bf16[2,1024,512]{2,1,0:T(8,128)(2,1)}, u32[]{:S(2)}, u32[]{:S(2)}) collective-permute-start(bf16[2,1024,512]{2,1,0:T(8,128)(2,1)} %get-tuple-element.57), channel_id=1, source_target_pairs={{0,8},{8,0},{16,24},{24,16},{1,9},{9,1},{17,25},{25,17},{2,10},{10... | collective-permute-start | bytes 6291464 | tf_op jit(solution)/shard_map/ppermute | solution.py:674
  283.7 25.7 %collective-permute-start.24 = (bf16[128,1024]{1,0:T(8,128)(2,1)S(1)}, bf16[128,1024]{1,0:T(8,128)(2,1)S(1)}, u32[]{:S(2)}, u32[]{:S(2)}) collective-permute-start(bf16[128,1024]{1,0:T(8,128)(2,1)S(1)} %get-tuple-element.67), channel_id=1, source_target_pairs={{0,4},{1,5},{2,6},{3,7},{4,0},{5,1},{6,2},{7,3},{8,12},{9,13},{10,... | collective-permute-start | bytes 786440 | tf_op jit(solution)/shard_map/ppermute | solution.py:674
  285.0 29.8 %collective-permute-start.25 = (bf16[128,1024]{1,0:T(8,128)(2,1)S(1)}, bf16[128,1024]{1,0:T(8,128)(2,1)S(1)}, u32[]{:S(2)}, u32[]{:S(2)}) collective-permute-start(bf16[128,1024]{1,0:T(8,128)(2,1)S(1)} %get-tuple-element.66), channel_id=1, source_target_pairs={{0,5},{1,4},{2,7},{3,6},{4,1},{5,0},{6,3},{7,2},{8,13},{9,12},{10,... | collective-permute-start | bytes 786440 | tf_op jit(solution)/shard_map/ppermute | solution.py:674
  288.1 27.2 %collective-permute-start.26 = (bf16[128,1024]{1,0:T(8,128)(2,1)S(1)}, bf16[128,1024]{1,0:T(8,128)(2,1)S(1)}, u32[]{:S(2)}, u32[]{:S(2)}) collective-permute-start(bf16[128,1024]{1,0:T(8,128)(2,1)S(1)} %get-tuple-element.65), channel_id=1, source_target_pairs={{0,6},{1,7},{2,4},{3,5},{4,2},{5,3},{6,0},{7,1},{8,14},{9,15},{10,... | collective-permute-start | bytes 786440 | tf_op jit(solution)/shard_map/ppermute | solution.py:674
  309.4 48.8 %collective-permute-start.39 = (bf16[2,1024,512]{2,1,0:T(8,128)(2,1)}, bf16[2,1024,512]{2,1,0:T(8,128)(2,1)}, u32[]{:S(2)}, u32[]{:S(2)}) collective-permute-start(bf16[2,1024,512]{2,1,0:T(8,128)(2,1)} %get-tuple-element.59), channel_id=1, source_target_pairs={{0,16},{8,24},{16,0},{24,8},{1,17},{9,25},{17,1},{25,9},{2,18},{10... | collective-permute-start | bytes 6291464 | tf_op jit(solution)/shard_map/ppermute | solution.py:674
  314.8 61.1 %collective-permute-start.33 = (bf16[2,256,2048]{2,1,0:T(8,128)(2,1)}, bf16[2,256,2048]{2,1,0:T(8,128)(2,1)}, u32[]{:S(2)}, u32[]{:S(2)}) collective-permute-start(bf16[2,256,2048]{2,1,0:T(8,128)(2,1)} %get-tuple-element.53), channel_id=1, source_target_pairs={{0,8},{8,0},{16,24},{24,16},{1,9},{9,1},{17,25},{25,17},{2,10},{10... | collective-permute-start | bytes 6291464 | tf_op jit(solution)/shard_map/ppermute | solution.py:674
  315.4 87.7 %collective-permute-start.35 = (bf16[2,256,2048]{2,1,0:T(8,128)(2,1)}, bf16[2,256,2048]{2,1,0:T(8,128)(2,1)}, u32[]{:S(2)}, u32[]{:S(2)}) collective-permute-start(bf16[2,256,2048]{2,1,0:T(8,128)(2,1)} %get-tuple-element.55), channel_id=1, source_target_pairs={{0,16},{8,24},{16,0},{24,8},{1,17},{9,25},{17,1},{25,9},{2,18},{10... | collective-permute-start | bytes 6291464 | tf_op jit(solution)/shard_map/ppermute | solution.py:674
  317.0 10.3 %collective-permute-start.27 = (bf16[128,1024]{1,0:T(8,128)(2,1)S(1)}, bf16[128,1024]{1,0:T(8,128)(2,1)S(1)}, u32[]{:S(2)}, u32[]{:S(2)}) collective-permute-start(bf16[128,1024]{1,0:T(8,128)(2,1)S(1)} %get-tuple-element.64), channel_id=1, source_target_pairs={{0,7},{1,6},{2,5},{3,4},{4,3},{5,2},{6,1},{7,0},{8,15},{9,14},{10,... | collective-permute-start | bytes 786440 | tf_op jit(solution)/shard_map/ppermute | solution.py:674
  327.3 99.8 %collective-permute-start.29 = (bf16[256,4224]{1,0:T(8,128)(2,1)}, bf16[256,4224]{1,0:T(8,128)(2,1)}, u32[]{:S(2)}, u32[]{:S(2)}) collective-permute-start(bf16[256,4224]{1,0:T(8,128)(2,1)} %slice.289), channel_id=1, source_target_pairs={{0,2},{1,3},{2,0},{3,1},{4,6},{5,7},{6,4},{7,5},{8,10},{9,11},{10,... | collective-permute-start | bytes 6488072 | tf_op jit(solution)/shard_map/ppermute | solution.py:674
  339.2 18.9 %copy-start.2 = (bf16[2,1024,512]{2,1,0:T(8,128)(2,1)S(1)}, bf16[2,1024,512]{2,1,0:T(8,128)(2,1)}, u32[]{:S(2)}) copy-start(bf16[2,1024,512]{2,1,0:T(8,128)(2,1)} %get-tuple-element.58) | copy-start | bytes 6291460
  339.2 36.7 %copy-start.5 = (bf16[2,256,2048]{2,1,0:T(8,128)(2,1)S(1)}, bf16[2,256,2048]{2,1,0:T(8,128)(2,1)}, u32[]{:S(2)}) copy-start(bf16[2,256,2048]{2,1,0:T(8,128)(2,1)} %get-tuple-element.52) | copy-start | bytes 6291460
  341.2 84.2 %collective-permute-start.38 = (bf16[1024,512]{1,0:T(8,128)(2,1)S(1)}, bf16[1024,512]{1,0:T(8,128)(2,1)S(1)}, u32[]{:S(2)}, u32[]{:S(2)}) collective-permute-start(bf16[1024,512]{1,0:T(8,128)(2,1)S(1)} %fusion.12), channel_id=1, source_target_pairs={{0,16},{8,24},{16,0},{24,8},{1,17},{9,25},{17,1},{25,9},{2,18},{10... | collective-permute-start | bytes 3145736 | tf_op jit(solution)/shard_map/ppermute | solution.py:674
  358.2 44.9 %copy-start.4 = (bf16[2,256,2048]{2,1,0:T(8,128)(2,1)S(1)}, bf16[2,256,2048]{2,1,0:T(8,128)(2,1)}, u32[]{:S(2)}) copy-start(bf16[2,256,2048]{2,1,0:T(8,128)(2,1)} %get-tuple-element.54) | copy-start | bytes 6291460
  359.9 133.0 %collective-permute-start.40 = (bf16[1024,512]{1,0:T(8,128)(2,1)S(1)}, bf16[1024,512]{1,0:T(8,128)(2,1)S(1)}, u32[]{:S(2)}, u32[]{:S(2)}) collective-permute-start(bf16[1024,512]{1,0:T(8,128)(2,1)S(1)} %fusion.13), channel_id=1, source_target_pairs={{0,8},{8,0},{16,24},{24,16},{1,9},{9,1},{17,25},{25,17},{2,10},{10... | collective-permute-start | bytes 3145736 | tf_op jit(solution)/shard_map/ppermute | solution.py:674
  375.9 51.2 %slice-start = ((s8[4325376]{0:T(1024)(128)(4,1)}), s8[4194304]{0:T(1024)(128)(4,1)S(1)}, s32[]{:S(2)}) async-start(s8[4325376]{0:T(1024)(128)(4,1)} %bitcast.41), calls=%async_computation | async-start | bytes 8388608
  377.7 47.8 %copy-start.3 = (bf16[2,1024,512]{2,1,0:T(8,128)(2,1)S(1)}, bf16[2,1024,512]{2,1,0:T(8,128)(2,1)}, u32[]{:S(2)}) copy-start(bf16[2,1024,512]{2,1,0:T(8,128)(2,1)} %get-tuple-element.56) | copy-start | bytes 6291460
  377.7 69.2 %collective-permute-start.34 = (bf16[256,2048]{1,0:T(8,128)(2,1)S(1)}, bf16[256,2048]{1,0:T(8,128)(2,1)S(1)}, u32[]{:S(2)}, u32[]{:S(2)}) collective-permute-start(bf16[256,2048]{1,0:T(8,128)(2,1)S(1)} %fusion.10), channel_id=1, source_target_pairs={{0,16},{8,24},{16,0},{24,8},{1,17},{9,25},{17,1},{25,9},{2,18},{10... | collective-permute-start | bytes 3145736 | tf_op jit(solution)/shard_map/ppermute | solution.py:674
  403.1 24.0 %slice-start.1 = ((s8[4325376]{0:T(1024)(128)(4,1)}), s8[131072]{0:T(1024)(128)(4,1)S(1)}, s32[]{:S(2)}) async-start(s8[4325376]{0:T(1024)(128)(4,1)} %bitcast.41), calls=%async_computation.1 | async-start | bytes 262144
  404.8 43.9 %collective-permute-start.36 = (bf16[256,2048]{1,0:T(8,128)(2,1)S(1)}, bf16[256,2048]{1,0:T(8,128)(2,1)S(1)}, u32[]{:S(2)}, u32[]{:S(2)}) collective-permute-start(bf16[256,2048]{1,0:T(8,128)(2,1)S(1)} %fusion.11), channel_id=1, source_target_pairs={{0,8},{8,0},{16,24},{24,16},{1,9},{9,1},{17,25},{25,17},{2,10},{10... | collective-permute-start | bytes 3145736 | tf_op jit(solution)/shard_map/ppermute | solution.py:674
  429.4 47.1 %collective-permute-start.30 = (bf16[128,4224]{1,0:T(8,128)(2,1)S(1)}, bf16[128,4224]{1,0:T(8,128)(2,1)S(1)}, u32[]{:S(2)}, u32[]{:S(2)}) collective-permute-start(bf16[128,4224]{1,0:T(8,128)(2,1)S(1)} %slice.291), channel_id=1, source_target_pairs={{0,4},{1,5},{2,6},{3,7},{4,0},{5,1},{6,2},{7,3},{8,12},{9,13},{10,... | collective-permute-start | bytes 3244040 | tf_op jit(solution)/shard_map/ppermute | solution.py:674
  476.8 14.3 %collective-permute-start.31 = (bf16[64,4224]{1,0:T(8,128)(2,1)S(1)}, bf16[64,4224]{1,0:T(8,128)(2,1)S(1)}, u32[]{:S(2)}, u32[]{:S(2)}) collective-permute-start(bf16[64,4224]{1,0:T(8,128)(2,1)S(1)} %slice.293), channel_id=1, source_target_pairs={{0,8},{8,0},{16,24},{24,16},{1,9},{9,1},{17,25},{25,17},{2,10},{10... | collective-permute-start | bytes 1622024 | tf_op jit(solution)/shard_map/ppermute | solution.py:674
  491.2 7.6 %collective-permute-start.32 = (bf16[32,4224]{1,0:T(8,128)(2,1)S(1)}, bf16[32,4224]{1,0:T(8,128)(2,1)S(1)}, u32[]{:S(2)}, u32[]{:S(2)}) collective-permute-start(bf16[32,4224]{1,0:T(8,128)(2,1)S(1)} %slice.295), channel_id=1, source_target_pairs={{0,16},{8,24},{16,0},{24,8},{1,17},{9,25},{17,1},{25,9},{2,18},{10... | collective-permute-start | bytes 811016 | tf_op jit(solution)/shard_map/ppermute | solution.py:674
  (4 other events, 6.7 us)
